TPU v7x, 128 devices: a whole 4x4x4 slice. The times are simulated.
128 devices in a mesh: req: 4 (over z), exp: 32 (over y, x, core).
Axes of the slice: x: 4, y: 4, z: 4, core: 2. Of those that a mesh axis runs over, the one named last changes fastest.
Arguments:
- hidden_in: bfloat16 [32, 512, 2048], P('exp'), may hold values from -6 to 6
- cache_keys: bfloat16 [32, 4096, 512], P('exp', None, 'req'), may hold values from -96 to 96
- cache_values: bfloat16 [32, 4096, 512], P('exp', None, 'req'), may hold values from -6 to 6
- cache_len: int32 [32], P('exp'), may hold values from 512 to 4096, as said below
- attn_gain: float32 [2048], replicated, may hold values from 0.25 to 1.75
- w_query: bfloat16 [2048, 4096], P('exp', 'req'), may hold values from -0.125 to 0.125
- w_key: bfloat16 [2048, 512], P('exp', 'req'), may hold values from -0.125 to 0.125
- w_value: bfloat16 [2048, 512], P('exp', 'req'), may hold values from -0.125 to 0.125
- q_gain: float32 [128], replicated, may hold values from 0.5 to 3
- k_gain: float32 [128], replicated, may hold values from 0.25 to 1.75
- w_out: bfloat16 [4096, 2048], P(('req', 'exp')), may hold values from -0.09375 to 0.09375
- moe_gain: float32 [2048], replicated, may hold values from 0.25 to 1.75
- expert_ids: int32 [32, 512, 8], P('exp', 'req'), may hold values from 0 to 127, all different within a row; in each aligned block of 128 rows (0 to 127, 128 to 255, ..., all dimensions but the last counted through in order) at most 12 rows name the same one
- expert_gates: float32 [32, 512, 8], P('exp', 'req'), may hold values from 0.05 to 0.5
- w_gate: bfloat16 [128, 2048, 768], P(('req', 'exp')), may hold values from -0.125 to 0.125
- w_up: bfloat16 [128, 2048, 768], P(('req', 'exp')), may hold values from -0.125 to 0.125
- w_down: bfloat16 [128, 768, 2048], P(('req', 'exp')), may hold values from -0.21875 to 0.21875
Outputs:
- hidden_out: bfloat16 [32, 512, 2048], P('exp', 'req')
- keys_out: bfloat16 [32, 4608, 512], P('exp', None, 'req')
- values_out: bfloat16 [32, 4608, 512], P('exp', None, 'req')
Inputs may be any that keep to these rules, and one draw needn't show every extreme that they name: `cache_len`: some request has exactly 4096 cached entries. `expert_ids`: each token names 8 different experts. In each aligned block of 128 tokens no expert is named more than 12 times, a bound that some block reaches.
All inputs are finite; a program needn't handle non-finite values.
Results may differ from a plain program's by a relative error of at most 0.014.
Values may be sent and summed in bfloat16 or wider, within the bound.
A program may use at most 128 MiB of HBM per device.

v0:
```python
import jax
import jax.numpy as jnp
from jax import lax
from jax.sharding import PartitionSpec as P

EPS = 1e-06
THETA = 1000000.0


def rms_norm(values, gain_vec):
    values = values.astype(jnp.float32)
    factor = lax.rsqrt(jnp.mean(values * values, axis=-1, keepdims=True) + EPS)
    return values * factor * gain_vec


def rotate(values, positions):
    half_dim = values.shape[-1] // 2
    frequency = THETA ** (-jnp.arange(half_dim, dtype=jnp.float32) * 2.0 / values.shape[-1])
    angles = positions.astype(jnp.float32)[:, None] * frequency[None, :]
    cosine = jnp.cos(angles)[:, None, :]
    sine_part = jnp.sin(angles)[:, None, :]
    lower_half = values[..., :half_dim]
    upper_half = values[..., half_dim:]
    return jnp.concatenate(
        [
            lower_half * cosine - upper_half * sine_part,
            upper_half * cosine + lower_half * sine_part,
        ],
        axis=-1,
    )


def finish(query_proj, key_proj, value_proj, q_gain, k_gain, positions):
    stretch_len = query_proj.shape[0]
    head_dim = q_gain.shape[0]
    queries = rotate(
        rms_norm(query_proj.reshape(stretch_len, -1, head_dim), q_gain), positions
    ).astype(jnp.bfloat16)
    fresh_keys = rotate(
        rms_norm(key_proj.reshape(stretch_len, -1, head_dim), k_gain), positions
    ).astype(jnp.bfloat16)
    return (
        queries.transpose(1, 0, 2),
        fresh_keys.reshape(stretch_len, -1),
        value_proj.astype(jnp.bfloat16),
    )


def context(cache, fresh, head_dim):
    joined = jnp.concatenate([cache, fresh], axis=0)
    return joined.reshape(joined.shape[0], -1, head_dim).transpose(1, 0, 2)


def visible(length, context_len, stretch_len):
    key_pos = jnp.arange(context_len + stretch_len, dtype=jnp.int32)[None, :]
    query_pos = jnp.arange(stretch_len, dtype=jnp.int32)[:, None]
    return (key_pos < length) | (key_pos >= context_len) & (key_pos - context_len <= query_pos)


def attend(queries, keys, values, visible_mask):
    group_size = queries.shape[0] // keys.shape[0]
    score_scale = queries.shape[2] ** (-0.5)

    def one_head(operands):
        query_head, head_index = operands
        key_block = keys[head_index // group_size]
        value_block = values[head_index // group_size]
        scores = jnp.dot(query_head, key_block.T, preferred_element_type=jnp.float32) * score_scale
        scores = jnp.where(visible_mask, scores, -1e30)
        row_peak = jnp.max(scores, axis=1, keepdims=True)
        weights = jnp.where(visible_mask, jnp.exp(scores - row_peak), 0.0)
        running = jnp.sum(weights, axis=1, keepdims=True)
        mixed = jnp.dot(
            weights.astype(jnp.bfloat16), value_block, preferred_element_type=jnp.float32
        )
        return (mixed / running).astype(jnp.bfloat16)

    return lax.map(one_head, (queries, jnp.arange(queries.shape[0], dtype=jnp.int32)))


def append(cache, fresh, length):
    span = cache.shape[0] + fresh.shape[0]
    padded = jnp.concatenate([cache, jnp.zeros_like(fresh)], axis=0)
    kept_rows = jnp.where(
        (jnp.arange(span, dtype=jnp.int32) < length)[:, None], padded, jnp.zeros_like(padded)
    )
    return lax.dynamic_update_slice(kept_rows, fresh, (length, jnp.zeros((), jnp.int32)))


def body(
    hidden_in,
    cache_keys,
    cache_values,
    cache_len,
    attn_gain,
    w_query,
    w_key,
    w_value,
    q_gain,
    k_gain,
    w_out,
    moe_gain,
    expert_ids,
    expert_gates,
    w_gate,
    w_up,
    w_down,
):
    tokens = hidden_in[0]
    stretch_len = tokens.shape[0]
    model_width = tokens.shape[1]
    length = cache_len[0]
    head_dim = q_gain.shape[0]
    normed = rms_norm(tokens, attn_gain).astype(jnp.bfloat16)
    query_proj = jnp.dot(
        normed,
        lax.all_gather(w_query, "exp", axis=0, tiled=True),
        preferred_element_type=jnp.float32,
    )
    key_proj = jnp.dot(
        normed, lax.all_gather(w_key, "exp", axis=0, tiled=True), preferred_element_type=jnp.float32
    )
    value_proj = jnp.dot(
        normed,
        lax.all_gather(w_value, "exp", axis=0, tiled=True),
        preferred_element_type=jnp.float32,
    )
    positions = length + jnp.arange(stretch_len, dtype=jnp.int32)
    queries, fresh_keys, fresh_values = finish(
        query_proj, key_proj, value_proj, q_gain, k_gain, positions
    )
    context_len = cache_keys.shape[1]
    visible_mask = visible(length, context_len, stretch_len)
    attended = attend(
        queries,
        context(cache_keys[0], fresh_keys, head_dim),
        context(cache_values[0], fresh_values, head_dim),
        visible_mask,
    )
    attended = attended.transpose(1, 0, 2).reshape(stretch_len, -1)
    groups = lax.axis_size("req")
    row_count = stretch_len // groups
    offset = lax.axis_index("req") * row_count
    block_in = attended
    partial_out = jnp.dot(
        block_in,
        lax.all_gather(w_out, "exp", axis=0, tiled=True),
        preferred_element_type=jnp.float32,
    )
    mixed = lax.psum_scatter(
        partial_out.astype(jnp.bfloat16), "req", scatter_dimension=0, tiled=True
    ).astype(jnp.float32)
    resident = lax.dynamic_slice_in_dim(tokens, offset, row_count, 0)
    after_attn = (resident.astype(jnp.float32) + mixed).astype(jnp.bfloat16)
    moe_in = rms_norm(after_attn, moe_gain).astype(jnp.bfloat16)
    routes = expert_ids[0]
    top_k = routes.shape[1]
    experts = groups * lax.axis_size("exp")
    capacity = 3 * top_k * row_count // (2 * experts)
    flat_ids = routes.reshape(-1)
    onehot = (flat_ids[:, None] == jnp.arange(experts, dtype=jnp.int32)[None, :]).astype(jnp.int32)
    slots = jnp.sum((jnp.cumsum(onehot, axis=0) - 1) * onehot, axis=1)
    target = flat_ids * capacity + slots
    sources = jnp.arange(row_count * top_k, dtype=jnp.int32) // top_k
    outgoing = (
        jnp.zeros((experts * capacity, model_width), jnp.bfloat16).at[target].set(moe_in[sources])
    )
    outgoing = outgoing.reshape(experts, capacity, model_width)
    block_in = lax.all_to_all(outgoing, ("req", "exp"), split_axis=0, concat_axis=0, tiled=True)
    flat_rows = block_in.reshape(-1, model_width)
    gate_proj = jnp.dot(flat_rows, w_gate[0], preferred_element_type=jnp.float32)
    up_proj = jnp.dot(flat_rows, w_up[0], preferred_element_type=jnp.float32)
    activated = (jax.nn.silu(gate_proj) * up_proj).astype(jnp.bfloat16)
    produced = jnp.dot(activated, w_down[0], preferred_element_type=jnp.float32).astype(
        jnp.bfloat16
    )
    returned = lax.all_to_all(
        produced.reshape(block_in.shape), ("req", "exp"), split_axis=0, concat_axis=0, tiled=True
    )
    picked = returned.reshape(experts * capacity, model_width)[target].reshape(
        row_count, top_k, model_width
    )
    combined = jnp.sum(picked.astype(jnp.float32) * expert_gates[0][:, :, None], axis=1)
    result_rows = (after_attn.astype(jnp.float32) + combined).astype(jnp.bfloat16)
    keys_out = append(cache_keys[0], fresh_keys, length)
    values_out = append(cache_values[0], fresh_values, length)
    return (result_rows[None], keys_out[None], values_out[None])


def solution(mesh):
    placed = (
        P("exp", None, None),
        P("exp", None, "req"),
        P("exp", None, "req"),
        P("exp"),
        P(),
        P("exp", "req"),
        P("exp", "req"),
        P("exp", "req"),
        P(),
        P(),
        P(("req", "exp"), None),
        P(),
        P("exp", "req", None),
        P("exp", "req", None),
        P(("req", "exp"), None, None),
        P(("req", "exp"), None, None),
        P(("req", "exp"), None, None),
    )
    return jax.shard_map(
        body,
        mesh=mesh,
        in_specs=placed,
        out_specs=(P("exp", "req", None), P("exp", None, "req"), P("exp", None, "req")),
        check_vma=False,
    )
```

profile of v0, /device:TPU:26, one launch (start us, length us, event | category | flops | bytes accessed | tf_op | source)
XLA Modules:
  0.0 569.8 jit_solution(8356940354222709908)
XLA Ops:
  9.4 2.1 fusion.36
  11.5 23.2 %all_gather.13 = bf16[2048,128]{1,0:T(8,128)(2,1)S(1)} all-gather(bf16[64,128]{1,0:T(8,128)(2,1)} %param.25), channel_id=1, replica_groups=mesh['req'=4,'exp'=32] {'exp'}, dimensions={0}, use_global_device_ids=true | all-gather | bytes 540672 | tf_op jit(solution)/shard_map/all_gather | solution.py:121
  34.8 2.5 multiply_reduce_fusion.1
  40.0 23.8 %all_gather.14 = bf16[2048,128]{1,0:T(8,128)(2,1)S(1)} all-gather(bf16[64,128]{1,0:T(8,128)(2,1)S(1)} %copy-done.15), channel_id=1, replica_groups=mesh['req'=4,'exp'=32] {'exp'}, dimensions={0}, use_global_device_ids=true | all-gather | bytes 540672 | tf_op jit(solution)/shard_map/all_gather | solution.py:125
  63.8 2.4 convolution_convert_fusion.2
  66.2 7.8 %select_bitcast_fusion = (bf16[1,4608,128]{2,1,0:T(8,128)(2,1)}, bf16[1,4608,128]{2,1,0:T(8,128)(2,1)}, bf16[1,4608,128]{2,1,0:T(8,128)(2,1)}, bf16[1,4608,128]{2,1,0:T(8,128)(2,1)}) fusion(bf16[4096,128]{1,0:T(8,128)(2,1)} %bitcast.122, pred[4608]{0:T(1024)(128)(4,1)S(1)} %get-tuple-element.187, bf16[512,128]{1,0:T(8,128)(2,1)S(1)} %convolution_convert_fusion.2, ...), kind=kLoop, calls=%fused_computation.58 | loop fusion | flops 5898240 | bytes 7082496 | tf_op jit(solution)/shard_map/broadcast_in_dim | solution.py:187
  74.0 6.5 %copy.25 = bf16[1024,2048]{1,0:T(8,128)(2,1)} copy(bf16[1024,2048]{0,1:T(8,128)(2,1)} %bitcast.120) | data formatting | bytes 8388608 | tf_op jit(solution)/shard_map/dot_general | solution.py:115
  80.5 5.3 multiply_reduce_fusion
  88.1 111.0 %while.12 = (s32[]{:T(128)}, bf16[8,512,128]{1,2,0:T(8,128)(2,1)}, bf16[8,512,128]{1,2,0:T(8,128)(2,1)}, bf16[1,4608,128]{2,1,0:T(8,128)(2,1)}, bf16[1,4608,128]...) while((s32[]{:T(128)}, bf16[8,512,128]{1,2,0:T(8,128)(2,1)}, ...), condition=%wide.region_6.7_spmd.clone, body=%wide.region_3.6_spmd.clone.sunk | while | flops 1259994112 | bytes 36270200 | solution.py:78
  88.3 4.5 fusion.90
  92.8 4.9 fusion.91
  97.7 3.7 fusion.92
  102.2 4.5 fusion.90
  106.6 4.9 fusion.91
  111.5 3.7 fusion.92
  116.0 4.5 fusion.90
  120.5 4.9 fusion.91
  125.4 3.7 fusion.92
  129.9 4.5 fusion.90
  134.4 4.9 fusion.91
  139.3 3.7 fusion.92
  143.7 4.5 fusion.90
  148.2 4.9 fusion.91
  153.1 3.7 fusion.92
  157.6 4.5 fusion.90
  162.1 4.9 fusion.91
  167.0 3.7 fusion.92
  171.4 4.5 fusion.90
  175.9 4.9 fusion.91
  180.8 3.7 fusion.92
  185.3 4.5 fusion.90
  189.8 4.9 fusion.91
  194.7 3.7 fusion.92
  199.2 6.2 %convolution_convert_fusion.1 = bf16[512,2048]{1,0:T(8,128)(2,1)} fusion(bf16[512,1024]{0,1:T(8,128)(2,1)} %bitcast.134, bf16[1024,2048]{1,0:T(8,128)(2,1)} %all-gather.5.cloned.1.call-done), kind=kOutput, calls=%fused_computation.46 | convolution fusion | flops 2148532224 | bytes 7340032 | tf_op jit(solution)/shard_map/dot_general | solution.py:145
  210.5 26.9 %reduce-scatter.2.cloned.1.call-done = bf16[128,2048]{1,0:T(8,128)(2,1)} async-done(((bf16[512,2048]{1,0:T(8,128)(2,1)}), bf16[128,2048]{1,0:T(8,128)(2,1)}) %reduce-scatter.2.cloned.1.call-update) | async-done | bytes 524304 | tf_op jit(solution)/shard_map/reduce_scatter | solution.py:150
  240.6 24.2 %scatter_custom_fusion = bf16[1536,2048]{1,0:T(8,128)(2,1)} fusion(s32[1024]{0:T(1024)S(1)} %bitcast.130, bf16[128,2048]{1,0:T(8,128)(2,1)} %fusion.55, s32[1024]{0:T(1024)S(1)} %broadcast_clamp_fusion.1, bf16[]{:T(256)} %constant.101.clone.1), kind=kCustom, calls=%fused_computation.39 | custom fusion | bytes 6291968 | tf_op jit(solution)/shard_map/scatter | solution.py:166
  264.8 10.6 %reshape.361 = bf16[128,12,2048]{2,1,0:T(8,128)(2,1)} reshape(bf16[1536,2048]{1,0:T(8,128)(2,1)} %scatter_custom_fusion) | data formatting | bytes 12582912 | tf_op jit(solution)/shard_map/reshape | solution.py:168
  275.4 103.2 %all_to_all.10 = bf16[128,12,2048]{2,1,0:T(8,128)(2,1)} all-to-all(bf16[128,12,2048]{2,1,0:T(8,128)(2,1)} %reshape.361), channel_id=1, replica_groups=mesh['req'=4,'exp'=32] {'req','exp'}, dimensions={0} | all-to-all | bytes 12582912 | tf_op jit(solution)/shard_map/all_to_all | solution.py:169
  378.6 10.7 %reshape.362 = bf16[1536,2048]{1,0:T(8,128)(2,1)} reshape(bf16[128,12,2048]{2,1,0:T(8,128)(2,1)} %all_to_all.10) | data formatting | bytes 12582912 | tf_op jit(solution)/shard_map/reshape | solution.py:170
  389.3 8.2 %fusion.45 = f32[1536,768]{1,0:T(8,128)S(1)} fusion(bf16[1536,2048]{1,0:T(8,128)(2,1)} %reshape.362, bf16[1,2048,768]{2,1,0:T(8,128)(2,1)} %param.33), kind=kOutput, calls=%fused_computation.43 | convolution fusion | flops 4831838208 | bytes 14155776 | tf_op jit(solution)/shard_map/dot_general | solution.py:171
  397.6 5.6 multiply_convert_fusion
  403.2 7.1 %convolution_convert_fusion = bf16[1536,2048]{1,0:T(8,128)(2,1)} fusion(bf16[1536,768]{1,0:T(8,128)(2,1)S(1)} %multiply_convert_fusion, bf16[1,768,2048]{2,1,0:T(8,128)(2,1)S(1)} %copy-done), kind=kOutput, calls=%fused_computation.28 | convolution fusion | flops 4834983936 | bytes 11796480 | tf_op jit(solution)/shard_map/dot_general | solution.py:174
  410.3 10.6 %reshape.363 = bf16[128,12,2048]{2,1,0:T(8,128)(2,1)} reshape(bf16[1536,2048]{1,0:T(8,128)(2,1)} %convolution_convert_fusion) | data formatting | bytes 12582912 | tf_op jit(solution)/shard_map/reshape | solution.py:178
  420.9 9.2 %all-to-all-start.1 = ((bf16[128,12,2048]{2,1,0:T(8,128)(2,1)}), bf16[128,12,2048]{2,1,0:T(8,128)(2,1)}, u32[]{:S(2)}, u32[]{:S(2)}) async-start(bf16[128,12,2048]{2,1,0:T(8,128)(2,1)} %reshape.363), calls=%async_computation.2 | async-start | bytes 16777216 | tf_op jit(solution)/shard_map/all_to_all | solution.py:177
  434.6 97.9 %all-to-all-done.1 = bf16[128,12,2048]{2,1,0:T(8,128)(2,1)} async-done(((bf16[128,12,2048]{2,1,0:T(8,128)(2,1)}), bf16[128,12,2048]{2,1,0:T(8,128)(2,1)}, u32[]{:S(2)}, u32[]{:S(2)}) %all-to-all-start.1) | async-done | bytes 6291488 | tf_op jit(solution)/shard_map/all_to_all | solution.py:177
  532.5 10.7 %reshape.364 = bf16[1536,2048]{1,0:T(8,128)(2,1)} reshape(bf16[128,12,2048]{2,1,0:T(8,128)(2,1)} %all-to-all-done.1) | data formatting | bytes 12582912 | tf_op jit(solution)/shard_map/reshape | solution.py:180
  543.2 12.4 %gather_fusion = bf16[1024,2048]{1,0:T(8,128)(2,1)} fusion(bf16[1536,2048]{1,0:T(8,128)(2,1)} %reshape.364, s32[1024]{0:T(1024)S(1)} %broadcast_clamp_fusion), kind=kCustom, calls=%fused_computation.1 | custom fusion | bytes 8392704 | tf_op jit(solution)/shard_map/gather | solution.py:180
  555.6 6.6 %fusion.33 = f32[128,2048]{1,0:T(8,128)S(1)} fusion(bf16[1024,2048]{1,0:T(8,128)(2,1)} %gather_fusion, f32[128,8]{1,0:T(8,128)S(1)} %copy-done.14), kind=kLoop, calls=%fused_computation.27 | loop fusion | flops 6029312 | bytes 5246976 | tf_op jit(solution)/shard_map/reduce_sum | solution.py:183
  (127 shorter events, 26.5 us)
Async XLA Ops:
  7.2 396.0 %copy-start = (bf16[1,768,2048]{2,1,0:T(8,128)(2,1)S(1)}, bf16[1,768,2048]{2,1,0:T(8,128)(2,1)}, u32[]{:S(2)}) copy-start(bf16[1,768,2048]{2,1,0:T(8,128)(2,1)} %param.35) | copy-start | bytes 9437188
  7.2 31.4 %copy-start.19 = (f32[128]{0:T(128)S(1)}, f32[128]{0:T(128)}, u32[]{:S(2)}) copy-start(f32[128]{0:T(128)} %param.28) | copy-start | bytes 1540
  7.2 66.8 %all-gather.3.cloned.1.call-start = ((), (), s32[]{:S(2)}) async-start(), calls=%async_computation.3 | async-start | bytes 4325376 | tf_op jit(solution)/shard_map/all_gather | solution.py:117
  7.9 191.2 %all-gather.5.cloned.1.call-start = ((), (), s32[]{:S(2)}) async-start(), calls=%async_computation.4 | async-start | bytes 4325376 | tf_op jit(solution)/shard_map/all_gather | solution.py:147
  8.7 228.7 %reduce-scatter.2.cloned.1.call-start = ((), (), s32[]{:S(2)}) async-start(), calls=%async_computation.5 | async-start | bytes 2621440 | tf_op jit(solution)/shard_map/reduce_scatter | solution.py:150
  9.4 30.6 %copy-start.15 = (bf16[64,128]{1,0:T(8,128)(2,1)S(1)}, bf16[64,128]{1,0:T(8,128)(2,1)}, u32[]{:S(2)}) copy-start(bf16[64,128]{1,0:T(8,128)(2,1)} %param.26) | copy-start | bytes 49156
  9.4 54.4 %copy-start.22 = (f32[2048]{0:T(1024)S(1)}, f32[2048]{0:T(1024)}, u32[]{:S(2)}) copy-start(f32[2048]{0:T(1024)} %param.23) | copy-start | bytes 24580
  39.2 0.6 copy-start.6
  39.2 0.6 copy-start.8
  66.2 14.3 %copy-start.10 = (bf16[512,128]{1,0:T(8,128)(2,1)}, bf16[512,128]{1,0:T(8,128)(2,1)S(1)}, u32[]{:S(2)}) copy-start(bf16[512,128]{1,0:T(8,128)(2,1)S(1)} %convolution_convert_fusion.2) | copy-start | bytes 393220
  80.4 5.3 copy-start.20
  85.7 0.9 copy-start.12
  85.8 1.0 copy-start.13
  92.8 4.9 copy-start.5
  106.6 4.9 copy-start.5
  120.5 4.9 copy-start.5
  134.4 4.9 copy-start.5
  148.2 4.9 copy-start.5
  162.1 4.9 copy-start.5
  175.9 4.9 copy-start.5
  189.8 4.9 copy-start.5
  199.2 6.2 %copy-start.16 = (s32[1,128,8]{1,2,0:T(8,128)S(1)}, s32[1,128,8]{1,2,0:T(8,128)}, u32[]{:S(2)}) copy-start(s32[1,128,8]{1,2,0:T(8,128)} %param.31) | copy-start | bytes 12292
  205.4 34.3 %copy-start.17 = (f32[2048]{0:T(1024)S(1)}, f32[2048]{0:T(1024)}, u32[]{:S(2)}) copy-start(f32[2048]{0:T(1024)} %param.30) | copy-start | bytes 24580
  206.0 0.8 copy-start.4
  238.8 0.8 copy-start.2
  389.3 8.2 %copy-start.1 = (bf16[1536,2048]{1,0:T(8,128)(2,1)S(1)}, bf16[1536,2048]{1,0:T(8,128)(2,1)}, u32[]{:S(2)}) copy-start(bf16[1536,2048]{1,0:T(8,128)(2,1)} %reshape.362) | copy-start | bytes 18874372
  389.3 8.2 %copy-start.21 = (bf16[1,2048,768]{2,1,0:T(8,128)(2,1)S(1)}, bf16[1,2048,768]{2,1,0:T(8,128)(2,1)}, u32[]{:S(2)}) copy-start(bf16[1,2048,768]{2,1,0:T(8,128)(2,1)} %param.34) | copy-start | bytes 9437188
  420.9 9.2 %copy-start.18 = (f32[1,128,8]{1,2,0:T(8,128)S(1)}, f32[1,128,8]{1,2,0:T(8,128)}, u32[]{:S(2)}) copy-start(f32[1,128,8]{1,2,0:T(8,128)} %param.32) | copy-start | bytes 12292
  420.9 10.0 %copy-start.7 = (bf16[512,1,64]{0,2,1:T(8,128)(2,1)S(1)}, bf16[512,1,64]{0,2,1:T(8,128)(2,1)}, u32[]{:S(2)}) copy-start(bf16[512,1,64]{0,2,1:T(8,128)(2,1)} %copy-done.6) | copy-start | bytes 196612
  420.9 10.0 %copy-start.9 = (bf16[512,1,64]{0,2,1:T(8,128)(2,1)S(1)}, bf16[512,1,64]{0,2,1:T(8,128)(2,1)}, u32[]{:S(2)}) copy-start(bf16[512,1,64]{0,2,1:T(8,128)(2,1)} %copy-done.8) | copy-start | bytes 196612
  420.9 11.9 %copy-start.11 = (bf16[512,128]{1,0:T(8,128)(2,1)S(1)}, bf16[512,128]{1,0:T(8,128)(2,1)}, u32[]{:S(2)}) copy-start(bf16[512,128]{1,0:T(8,128)(2,1)} %copy-done.10) | copy-start | bytes 393220
  420.9 111.6 %all-to-all-start.1 = ((bf16[128,12,2048]{2,1,0:T(8,128)(2,1)}), bf16[128,12,2048]{2,1,0:T(8,128)(2,1)}, u32[]{:S(2)}, u32[]{:S(2)}) async-start(bf16[128,12,2048]{2,1,0:T(8,128)(2,1)} %reshape.363), calls=%async_computation.2 | async-start | bytes 16777216 | tf_op jit(solution)/shard_map/all_to_all | solution.py:177
  543.2 12.4 %copy-start.14 = (f32[128,8]{1,0:T(8,128)S(1)}, f32[128,8]{1,0:T(8,128)}, u32[]{:S(2)}) copy-start(f32[128,8]{1,0:T(8,128)} %copy.34) | copy-start | bytes 12292
  555.6 6.6 %copy-start.3 = (bf16[128,2048]{1,0:T(8,128)(2,1)S(1)}, bf16[128,2048]{1,0:T(8,128)(2,1)}, u32[]{:S(2)}) copy-start(bf16[128,2048]{1,0:T(8,128)(2,1)} %copy-done.2) | copy-start | bytes 1572868
Sparse Core Ops, SparseCore 0:
  10.3 46.5 all-gather.2
  59.1 45.2 all-gather.4
  205.5 31.7 reduce-scatter.1
where the time goes:
time: 580 us; the launch traced here: 570 us
  blocking collectives  150 us (26%)
  waiting for transfers between devices  126 us (22%)
  matrix products  102 us (18%)
  local copies, waits for them, and re-layouts  101 us (17%)
  other arithmetic  65.5 us (11%)
  between operations  15 us (3%)
  starting transfers between devices  9.33 us (2%)
    all_to_all x1, blocking collectives, body(): lax.all_to_all(outgoing, ('req', 'exp'), split_axis=0, concat_axis=0, til...  103 us
    all_to_all x1, waiting for transfers between devices, body(): lax.all_to_all(produced.reshape(block_in.shape), ('req', 'exp'), split_ax...  97.9 us
    reduce_sum x8, other arithmetic, one_head(): running = jnp.sum(weights, axis=1, keepdims=True)  39.1 us
    dot_general x8, matrix products, one_head(): jnp.dot(query_head, key_block.T, preferred_element_type=jnp.float32)  35.7 us
    dot_general x8, matrix products, one_head(): jnp.dot(weights.astype(jnp.bfloat16), value_block, preferred_element_type...  29.4 us
    reduce_scatter x1, waiting for transfers between devices, body(): lax.psum_scatter(partial_out.astype(jnp.bfloat16), 'req', scatter_dimensi...  26.9 us
    scatter x1, local copies, waits for them, and re-layouts, body(): jnp.zeros((experts * capacity, model_width), jnp.bfloat16).at[target]  24.2 us
    all_gather x1, blocking collectives, body(): lax.all_gather(w_value, 'exp', axis=0, tiled=True)  23.8 us
  transfers between devices with their start and end apart: 4, of which 2 were waited for; matrix products, arithmetic and copies ran while one was open for 26% of the time, Pallas kernels for 0%

commit v1 on v0

--- a/solution.py
+++ b/solution.py
@@ -1,6 +1,11 @@
+import functools
+import math
+
 import jax
 import jax.numpy as jnp
 from jax import lax
+from jax.experimental import pallas as pl
+from jax.experimental.pallas import tpu as pltpu
 from jax.sharding import PartitionSpec as P
 
 EPS = 1e-06
@@ -46,36 +51,74 @@
     )
 
 
-def context(cache, fresh, head_dim):
-    joined = jnp.concatenate([cache, fresh], axis=0)
-    return joined.reshape(joined.shape[0], -1, head_dim).transpose(1, 0, 2)
-
-
-def visible(length, context_len, stretch_len):
-    key_pos = jnp.arange(context_len + stretch_len, dtype=jnp.int32)[None, :]
-    query_pos = jnp.arange(stretch_len, dtype=jnp.int32)[:, None]
-    return (key_pos < length) | (key_pos >= context_len) & (key_pos - context_len <= query_pos)
-
-
-def attend(queries, keys, values, visible_mask):
-    group_size = queries.shape[0] // keys.shape[0]
-    score_scale = queries.shape[2] ** (-0.5)
-
-    def one_head(operands):
-        query_head, head_index = operands
-        key_block = keys[head_index // group_size]
-        value_block = values[head_index // group_size]
-        scores = jnp.dot(query_head, key_block.T, preferred_element_type=jnp.float32) * score_scale
-        scores = jnp.where(visible_mask, scores, -1e30)
-        row_peak = jnp.max(scores, axis=1, keepdims=True)
-        weights = jnp.where(visible_mask, jnp.exp(scores - row_peak), 0.0)
-        running = jnp.sum(weights, axis=1, keepdims=True)
-        mixed = jnp.dot(
-            weights.astype(jnp.bfloat16), value_block, preferred_element_type=jnp.float32
-        )
-        return (mixed / running).astype(jnp.bfloat16)
-
-    return lax.map(one_head, (queries, jnp.arange(queries.shape[0], dtype=jnp.int32)))
+def attention_body(exp_scale, len_ref, q_ref, k_ref, v_ref, fk_ref, fv_ref, o_ref, kaug, vaug):
+    block = pl.program_id(0)
+    length = len_ref[0]
+    heads, tokens, width = q_ref.shape
+    cached = k_ref.shape[0]
+    fresh = fk_ref.shape[0]
+
+    @pl.when(block == 0)
+    def _():
+        kaug[0:cached, 0:width] = k_ref[...]
+        kaug[cached:, 0:width] = fk_ref[...]
+        row = lax.broadcasted_iota(jnp.int32, (cached + fresh, width), 0)
+        lane = lax.broadcasted_iota(jnp.int32, (cached + fresh, width), 1)
+        hidden = (lane == 0) & (row >= length) & (row < cached)
+        kaug[:, width:] = jnp.where(hidden, -1e30, 0.0).astype(jnp.bfloat16)
+        vaug[0:cached, 0:width] = v_ref[...]
+        vaug[cached:, 0:width] = fv_ref[...]
+        vaug[:, width:] = jnp.ones((cached + fresh, width), jnp.bfloat16)
+
+    rows = heads * tokens
+    queries = q_ref[...].reshape(rows, width)
+    widened = jnp.concatenate([queries, jnp.ones((rows, width), jnp.bfloat16)], axis=1)
+    dims = (((1,), (1,)), ((), ()))
+    old = lax.dot_general(widened, kaug[0:cached, :], dims, preferred_element_type=jnp.float32)
+    new = lax.dot_general(
+        queries, kaug[cached:, 0:width], dims, preferred_element_type=jnp.float32
+    )
+    token = lax.broadcasted_iota(jnp.int32, (rows, fresh), 0) % tokens + block * tokens
+    new = jnp.where(lax.broadcasted_iota(jnp.int32, (rows, fresh), 1) <= token, new, -1e30)
+    peak = jnp.maximum(
+        jnp.max(old, axis=1, keepdims=True), jnp.max(new, axis=1, keepdims=True)
+    )
+    old = jnp.exp2((old - peak) * exp_scale).astype(jnp.bfloat16)
+    new = jnp.exp2((new - peak) * exp_scale).astype(jnp.bfloat16)
+    mixed = jnp.dot(old, vaug[0:cached, :], preferred_element_type=jnp.float32) + jnp.dot(
+        new, vaug[cached:, :], preferred_element_type=jnp.float32
+    )
+    mixed = (mixed[:, :width] / mixed[:, width:]).astype(jnp.bfloat16)
+    for head in range(heads):
+        o_ref[:, head * width : (head + 1) * width] = mixed[head * tokens : (head + 1) * tokens]
+
+
+def attend(queries, cache_k, cache_v, fresh_k, fresh_v, length, tokens=128):
+    heads, stretch_len, width = queries.shape
+    span = cache_k.shape[0] + fresh_k.shape[0]
+    whole = lambda arr: pl.BlockSpec(arr.shape, lambda i, n: (0, 0))
+    return pl.pallas_call(
+        functools.partial(attention_body, width ** -0.5 * math.log2(math.e)),
+        out_shape=jax.ShapeDtypeStruct((stretch_len, heads * width), jnp.bfloat16),
+        grid_spec=pltpu.PrefetchScalarGridSpec(
+            num_scalar_prefetch=1,
+            grid=(stretch_len // tokens,),
+            in_specs=[
+                pl.BlockSpec((heads, tokens, width), lambda i, n: (0, i, 0)),
+                whole(cache_k),
+                whole(cache_v),
+                whole(fresh_k),
+                whole(fresh_v),
+            ],
+            out_specs=pl.BlockSpec((tokens, heads * width), lambda i, n: (i, 0)),
+            scratch_shapes=[
+                pltpu.VMEM((span, 2 * width), jnp.bfloat16),
+                pltpu.VMEM((span, 2 * width), jnp.bfloat16),
+            ],
+        ),
+        compiler_params=pltpu.CompilerParams(vmem_limit_bytes=58 << 20),
+        name="attend",
+    )(length, queries, cache_k, cache_v, fresh_k, fresh_v)
 
 
 def append(cache, fresh, length):
@@ -112,32 +155,19 @@
     length = cache_len[0]
     head_dim = q_gain.shape[0]
     normed = rms_norm(tokens, attn_gain).astype(jnp.bfloat16)
-    query_proj = jnp.dot(
-        normed,
-        lax.all_gather(w_query, "exp", axis=0, tiled=True),
-        preferred_element_type=jnp.float32,
-    )
-    key_proj = jnp.dot(
-        normed, lax.all_gather(w_key, "exp", axis=0, tiled=True), preferred_element_type=jnp.float32
-    )
-    value_proj = jnp.dot(
-        normed,
-        lax.all_gather(w_value, "exp", axis=0, tiled=True),
-        preferred_element_type=jnp.float32,
-    )
+    widths = (w_query.shape[1], w_key.shape[1], w_value.shape[1])
+    w_all = lax.all_gather(
+        jnp.concatenate([w_query, w_key, w_value], axis=1), "exp", axis=0, tiled=True
+    )
+    proj = jnp.dot(normed, w_all, preferred_element_type=jnp.float32)
+    query_proj = proj[:, : widths[0]]
+    key_proj = proj[:, widths[0] : widths[0] + widths[1]]
+    value_proj = proj[:, widths[0] + widths[1] :]
     positions = length + jnp.arange(stretch_len, dtype=jnp.int32)
     queries, fresh_keys, fresh_values = finish(
         query_proj, key_proj, value_proj, q_gain, k_gain, positions
     )
-    context_len = cache_keys.shape[1]
-    visible_mask = visible(length, context_len, stretch_len)
-    attended = attend(
-        queries,
-        context(cache_keys[0], fresh_keys, head_dim),
-        context(cache_values[0], fresh_values, head_dim),
-        visible_mask,
-    )
-    attended = attended.transpose(1, 0, 2).reshape(stretch_len, -1)
+    attended = attend(queries, cache_keys[0], cache_values[0], fresh_keys, fresh_values, cache_len)
     groups = lax.axis_size("req")
     row_count = stretch_len // groups
     offset = lax.axis_index("req") * row_count

time: 580 us -> 510 us (0.88)
  matrix products: 102 us -> 33.1 us
  Pallas kernels: 0 us -> 50.8 us
  blocking collectives: 150 us -> 103 us
  waiting for transfers between devices: 126 us -> 163 us
  other arithmetic: 65.5 us -> 32.6 us
    dot_general x19 -> x1, matrix products: 75.3 us -> 6.06 us  [body(): proj = jnp.dot(normed, w_all, preferred_element_type=jnp.float32)]
    pallas_call x0 -> x1, Pallas kernels: none -> 50.8 us  [attend(): pl.pallas_call(functools.partial(attention_body, width ** (-0.5) * math.l...]
    all_gather x2 -> x0, blocking collectives: 47 us -> none  [the longest x1 23.8 us: body(): lax.all_gather(w_value, 'exp', axis=0, tiled=True)]
    all_gather x1, waiting for transfers between devices: 0.01 us -> 43.8 us  [body(): lax.all_gather(jnp.concatenate([w_query, w_key, w_value], axis=1), 'exp',...]
    reduce_sum x8 -> x0, other arithmetic: 39.1 us -> none  [one_head(): running = jnp.sum(weights, axis=1, keepdims=True)]
    dot_general x1 -> x0, local copies, waits for them, and re-layouts: 6.48 us -> none  [body(): jnp.dot(normed, lax.all_gather(w_query, 'exp', axis=0, tiled=True), prefe...]
    dynamic_update_slice x16 -> x0, local copies, waits for them, and re-layouts: 6.29 us -> none  [attend(): lax.map(one_head, (queries, jnp.arange(queries.shape[0], dtype=jnp.int32)))]
  transfers between devices with their start and end apart: 4 -> 4, of which waited for: 2 -> 3; matrix products, arithmetic and copies ran while one was open for 26% -> 8% of each run, Pallas kernels for 0% -> 10%
where the time goes in v1:
time: 510 us; the launch traced here: 503 us
  waiting for transfers between devices  163 us (32%)
  blocking collectives  103 us (20%)
  local copies, waits for them, and re-layouts  96.3 us (19%)
  Pallas kernels  50.8 us (10%)
  matrix products  33.1 us (6%)
  other arithmetic  32.6 us (6%)
  between operations  15 us (3%)
  starting transfers between devices  9.35 us (2%)
    all_to_all x1, blocking collectives, body(): lax.all_to_all(outgoing, ('req', 'exp'), split_axis=0, concat_axis=0, til...  103 us
    all_to_all x1, waiting for transfers between devices, body(): lax.all_to_all(produced.reshape(block_in.shape), ('req', 'exp'), split_ax...  92.2 us
    pallas_call x1, Pallas kernels, attend(): pl.pallas_call(functools.partial(attention_body, width ** (-0.5) * math.l...  50.8 us
    all_gather x1, waiting for transfers between devices, body(): lax.all_gather(jnp.concatenate([w_query, w_key, w_value], axis=1), 'exp',...  43.8 us
    reduce_scatter x1, waiting for transfers between devices, body(): lax.psum_scatter(partial_out.astype(jnp.bfloat16), 'req', scatter_dimensi...  26.1 us
    scatter x1, local copies, waits for them, and re-layouts, body(): jnp.zeros((experts * capacity, model_width), jnp.bfloat16).at[target]  24.1 us
    gather x1, local copies, waits for them, and re-layouts, body(): returned.reshape(experts * capacity, model_width)[target]  12.4 us
    reshape x1, local copies, waits for them, and re-layouts, body(): flat_rows = block_in.reshape(-1, model_width)  10.7 us
  transfers between devices with their start and end apart: 4, of which 3 were waited for; matrix products, arithmetic and copies ran while one was open for 8% of the time, Pallas kernels for 10%

profile of v1, /device:TPU:26, one launch (start us, length us, event | category | flops | bytes accessed | tf_op | source)
XLA Modules:
  0.0 502.8 jit_solution(17897464530636825016)
XLA Ops:
  7.2 1.8 pad_maximum_fusion
  9.1 0.7 all-gather.5.cloned.1.call-update
  10.5 2.1 fusion.1
  12.6 1.8 multiply_cosine_fusion.1
  14.4 43.8 %all-gather.3.cloned.1.call-done = bf16[2048,1280]{1,0:T(8,128)(2,1)} async-done(((bf16[64,1280]{1,0:T(8,128)(2,1)}), bf16[2048,1280]{1,0:T(8,128)(2,1)}) %all-gather.3.cloned.1.call-update) | async-done | bytes 5242896 | tf_op jit(solution)/shard_map/all_gather | solution.py:159
  58.2 6.1 %fusion.11 = f32[512,1280]{1,0:T(8,128)S(1)} fusion(bf16[2048,1280]{1,0:T(8,128)(2,1)} %all-gather.3.cloned.1.call-done, bf16[1,512,2048]{2,1,0:T(8,128)(2,1)} %param.17, f32[2048]{0:T(1024)} %param.21, f32[512]{0:T(512)S(1)} %add_rsqrt_fusion.2), kind=kOutput, calls=%fused_computation.20 | convolution fusion | flops 2688548864 | bytes 9971712 | tf_op jit(solution)/shard_map/dot_general | solution.py:162
  64.3 0.7 slice.64.fv_ref
  65.0 0.8 copy-done.5
  65.8 1.6 slice.41
  67.4 2.9 copy.21
  70.3 2.9 copy.22
  73.3 1.2 multiply_reduce_fusion.1
  74.5 1.1 multiply_bitcast_fusion
  75.6 1.2 fusion.30
  76.9 0.8 pad_maximum_fusion.1.fk_ref
  77.6 1.9 multiply_reduce_fusion
  79.5 0.7 multiply_multiply_fusion
  80.3 0.8 subtract_convert_fusion
  81.0 1.5 maximum_bitcast_fusion.q_ref
  82.6 50.8 %attend.1 = bf16[512,1024]{1,0:T(8,128)(2,1)} custom-call(s32[1]{0:T(128)} %copy.31.len_ref, bf16[8,512,128]{2,1,0:T(8,128)(2,1)} %maximum_bitcast_fusion.q_ref, bf16[4096,128]{1,0:T(8,128)(2,1)} %bitcast.69, bf16[4096,128]{1,0:T(8,128)(2,1)} %bitcast.71, bf16[512,128]{1,0:T(8,128)(2,1)} %pad_maximum_fusion.1.fk_ref, bf16[512,128]{1,0:T(8,128)(2,1)} %slice.64.fv_ref), custom_call_target="tpu_custom_call" | custom-call | tf_op jit(solution)/shard_map/attend/pallas_call | solution.py:100
  133.5 6.2 %convolution_convert_fusion.1 = bf16[512,2048]{1,0:T(8,128)(2,1)} fusion(bf16[512,1024]{1,0:T(8,128)(2,1)} %attend.1, bf16[1024,2048]{1,0:T(8,128)(2,1)} %all-gather.5.cloned.1.call-done), kind=kOutput, calls=%fused_computation.19 | convolution fusion | flops 2148532224 | bytes 7340032 | tf_op jit(solution)/shard_map/dot_general | solution.py:175
  140.5 0.8 copy-done.6
  141.3 1.1 add_add_fusion
  142.4 0.9 copy.27
  143.3 1.4 fusion.22
  144.8 26.1 %reduce-scatter.2.cloned.1.call-done = bf16[128,2048]{1,0:T(8,128)(2,1)} async-done(((bf16[512,2048]{1,0:T(8,128)(2,1)}), bf16[128,2048]{1,0:T(8,128)(2,1)}) %reduce-scatter.2.cloned.1.call-update) | async-done | bytes 524304 | tf_op jit(solution)/shard_map/reduce_scatter | solution.py:180
  170.8 1.5 fusion.16
  172.3 0.8 copy-done.3
  173.1 1.0 fusion.18
  174.1 24.1 %scatter_custom_fusion = bf16[1536,2048]{1,0:T(8,128)(2,1)} fusion(s32[1024]{0:T(1024)S(1)} %bitcast.78, bf16[128,2048]{1,0:T(8,128)(2,1)} %fusion.18, s32[1024]{0:T(1024)S(1)} %broadcast_clamp_fusion.1, bf16[]{:T(256)} %constant.68.clone.1), kind=kCustom, calls=%fused_computation.12 | custom fusion | bytes 6291968 | tf_op jit(solution)/shard_map/scatter | solution.py:196
  198.3 10.6 %reshape.328 = bf16[128,12,2048]{2,1,0:T(8,128)(2,1)} reshape(bf16[1536,2048]{1,0:T(8,128)(2,1)} %scatter_custom_fusion) | data formatting | bytes 12582912 | tf_op jit(solution)/shard_map/reshape | solution.py:198
  208.9 102.8 %all_to_all.10 = bf16[128,12,2048]{2,1,0:T(8,128)(2,1)} all-to-all(bf16[128,12,2048]{2,1,0:T(8,128)(2,1)} %reshape.328), channel_id=1, replica_groups=mesh['req'=4,'exp'=32] {'req','exp'}, dimensions={0} | all-to-all | bytes 12582912 | tf_op jit(solution)/shard_map/all_to_all | solution.py:199
  311.6 10.7 %reshape.329 = bf16[1536,2048]{1,0:T(8,128)(2,1)} reshape(bf16[128,12,2048]{2,1,0:T(8,128)(2,1)} %all_to_all.10) | data formatting | bytes 12582912 | tf_op jit(solution)/shard_map/reshape | solution.py:200
  322.3 8.2 %fusion.8 = f32[1536,768]{1,0:T(8,128)S(1)} fusion(bf16[1536,2048]{1,0:T(8,128)(2,1)} %reshape.329, bf16[1,2048,768]{2,1,0:T(8,128)(2,1)} %param.31), kind=kOutput, calls=%fused_computation.16 | convolution fusion | flops 4831838208 | bytes 14155776 | tf_op jit(solution)/shard_map/dot_general | solution.py:201
  330.6 5.6 %multiply_convert_fusion = bf16[1536,768]{1,0:T(8,128)(2,1)S(1)} fusion(f32[1536,768]{1,0:T(8,128)S(1)} %fusion.8, bf16[1536,2048]{1,0:T(8,128)(2,1)S(1)} %copy-done.2, bf16[1,2048,768]{2,1,0:T(8,128)(2,1)S(1)} %copy-done.15), kind=kOutput, calls=%fused_computation.8 | convolution fusion | flops 4838916096 | bytes 16515072 | tf_op jit(solution)/shard_map/dot_general | solution.py:202
  336.2 7.1 %convolution_convert_fusion = bf16[1536,2048]{1,0:T(8,128)(2,1)} fusion(bf16[1536,768]{1,0:T(8,128)(2,1)S(1)} %multiply_convert_fusion, bf16[1,768,2048]{2,1,0:T(8,128)(2,1)S(1)} %copy-done), kind=kOutput, calls=%fused_computation.5 | convolution fusion | flops 4834983936 | bytes 11796480 | tf_op jit(solution)/shard_map/dot_general | solution.py:204
  343.3 10.6 %reshape.330 = bf16[128,12,2048]{2,1,0:T(8,128)(2,1)} reshape(bf16[1536,2048]{1,0:T(8,128)(2,1)} %convolution_convert_fusion) | data formatting | bytes 12582912 | tf_op jit(solution)/shard_map/reshape | solution.py:208
  353.9 9.2 %all-to-all-start.1 = ((bf16[128,12,2048]{2,1,0:T(8,128)(2,1)}), bf16[128,12,2048]{2,1,0:T(8,128)(2,1)}, u32[]{:S(2)}, u32[]{:S(2)}) async-start(bf16[128,12,2048]{2,1,0:T(8,128)(2,1)} %reshape.330), calls=%async_computation.2 | async-start | bytes 16777216 | tf_op jit(solution)/shard_map/all_to_all | solution.py:207
  363.1 0.7 copy.28
  363.9 4.9 select_bitcast_fusion
  368.8 1.0 slice_bitcast_fusion.1
  369.8 1.7 dynamic_update_slice.9
  371.5 1.7 dynamic_update_slice.8
  373.2 92.2 %all-to-all-done.1 = bf16[128,12,2048]{2,1,0:T(8,128)(2,1)} async-done(((bf16[128,12,2048]{2,1,0:T(8,128)(2,1)}), bf16[128,12,2048]{2,1,0:T(8,128)(2,1)}, u32[]{:S(2)}, u32[]{:S(2)}) %all-to-all-start.1) | async-done | bytes 6291488 | tf_op jit(solution)/shard_map/all_to_all | solution.py:207
  465.5 10.7 %reshape.331 = bf16[1536,2048]{1,0:T(8,128)(2,1)} reshape(bf16[128,12,2048]{2,1,0:T(8,128)(2,1)} %all-to-all-done.1) | data formatting | bytes 12582912 | tf_op jit(solution)/shard_map/reshape | solution.py:210
  476.1 12.4 %gather_fusion = bf16[1024,2048]{1,0:T(8,128)(2,1)} fusion(bf16[1536,2048]{1,0:T(8,128)(2,1)} %reshape.331, s32[1024]{0:T(1024)S(1)} %broadcast_clamp_fusion), kind=kCustom, calls=%fused_computation.1 | custom fusion | bytes 8392704 | tf_op jit(solution)/shard_map/gather | solution.py:210
  488.6 6.6 %fusion = f32[128,2048]{1,0:T(8,128)S(1)} fusion(bf16[1024,2048]{1,0:T(8,128)(2,1)} %gather_fusion, f32[128,8]{1,0:T(8,128)S(1)} %copy-done.9), kind=kLoop, calls=%fused_computation.4 | loop fusion | flops 6029312 | bytes 5246976 | tf_op jit(solution)/shard_map/reduce_sum | solution.py:213
  495.2 0.9 fusion.21
  (58 shorter events, 1.2 us)
Async XLA Ops:
  7.2 329.0 %copy-start = (bf16[1,768,2048]{2,1,0:T(8,128)(2,1)S(1)}, bf16[1,768,2048]{2,1,0:T(8,128)(2,1)}, u32[]{:S(2)}) copy-start(bf16[1,768,2048]{2,1,0:T(8,128)(2,1)} %param.33) | copy-start | bytes 9437188
  7.2 51.1 %all-gather.3.cloned.1.call-start = ((), (), s32[]{:S(2)}) async-start(), calls=%async_computation.3 | async-start | bytes 5406720 | tf_op jit(solution)/shard_map/all_gather | solution.py:159
  9.0 124.4 %all-gather.5.cloned.1.call-start = ((), (), s32[]{:S(2)}) async-start(), calls=%async_computation.4 | async-start | bytes 4325376 | tf_op jit(solution)/shard_map/all_gather | solution.py:177
  9.8 161.1 %reduce-scatter.2.cloned.1.call-start = ((), (), s32[]{:S(2)}) async-start(), calls=%async_computation.5 | async-start | bytes 2621440 | tf_op jit(solution)/shard_map/reduce_scatter | solution.py:180
  64.3 1.5 copy-start.5
  67.4 7.1 %copy-start.13 = (f32[128]{0:T(128)S(1)}, f32[128]{0:T(128)}, u32[]{:S(2)}) copy-start(f32[128]{0:T(128)} %param.26) | copy-start | bytes 1540
  70.3 9.2 %copy-start.14 = (f32[128]{0:T(128)S(1)}, f32[128]{0:T(128)}, u32[]{:S(2)}) copy-start(f32[128]{0:T(128)} %param.25) | copy-start | bytes 1540
  73.3 6.3 %copy-start.1 = (f32[512,8,128]{2,0,1:T(8,128)S(1)}, f32[512,8,128]{2,0,1:T(8,128)}, u32[]{:S(2)}) copy-start(f32[512,8,128]{2,0,1:T(8,128)} %copy.22) | copy-start | bytes 6291460
  73.3 7.0 %copy-start.7 = (f32[512,64]{1,0:T(8,128)S(1)}, f32[512,64]{1,0:T(8,128)}, u32[]{:S(2)}) copy-start(f32[512,64]{1,0:T(8,128)} %get-tuple-element.11) | copy-start | bytes 393220
  73.3 7.0 %copy-start.8 = (f32[512,64]{1,0:T(8,128)S(1)}, f32[512,64]{1,0:T(8,128)}, u32[]{:S(2)}) copy-start(f32[512,64]{1,0:T(8,128)} %get-tuple-element.12) | copy-start | bytes 393220
  133.4 6.3 %copy-start.10 = (s32[1,128,8]{1,2,0:T(8,128)S(1)}, s32[1,128,8]{1,2,0:T(8,128)}, u32[]{:S(2)}) copy-start(s32[1,128,8]{1,2,0:T(8,128)} %param.29) | copy-start | bytes 12292
  139.6 33.5 %copy-start.11 = (f32[2048]{0:T(1024)S(1)}, f32[2048]{0:T(1024)}, u32[]{:S(2)}) copy-start(f32[2048]{0:T(1024)} %param.28) | copy-start | bytes 24580
  140.5 0.8 copy-start.6
  172.3 0.8 copy-start.3
  322.3 8.2 %copy-start.2 = (bf16[1536,2048]{1,0:T(8,128)(2,1)S(1)}, bf16[1536,2048]{1,0:T(8,128)(2,1)}, u32[]{:S(2)}) copy-start(bf16[1536,2048]{1,0:T(8,128)(2,1)} %reshape.329) | copy-start | bytes 18874372
  322.3 8.2 %copy-start.15 = (bf16[1,2048,768]{2,1,0:T(8,128)(2,1)S(1)}, bf16[1,2048,768]{2,1,0:T(8,128)(2,1)}, u32[]{:S(2)}) copy-start(bf16[1,2048,768]{2,1,0:T(8,128)(2,1)} %param.32) | copy-start | bytes 9437188
  353.9 9.2 %copy-start.12 = (f32[1,128,8]{1,2,0:T(8,128)S(1)}, f32[1,128,8]{1,2,0:T(8,128)}, u32[]{:S(2)}) copy-start(f32[1,128,8]{1,2,0:T(8,128)} %param.30) | copy-start | bytes 12292
  353.9 111.6 %all-to-all-start.1 = ((bf16[128,12,2048]{2,1,0:T(8,128)(2,1)}), bf16[128,12,2048]{2,1,0:T(8,128)(2,1)}, u32[]{:S(2)}, u32[]{:S(2)}) async-start(bf16[128,12,2048]{2,1,0:T(8,128)(2,1)} %reshape.330), calls=%async_computation.2 | async-start | bytes 16777216 | tf_op jit(solution)/shard_map/all_to_all | solution.py:207
  476.1 12.4 %copy-start.9 = (f32[128,8]{1,0:T(8,128)S(1)}, f32[128,8]{1,0:T(8,128)}, u32[]{:S(2)}) copy-start(f32[128,8]{1,0:T(8,128)} %copy.28) | copy-start | bytes 12292
  488.6 6.6 %copy-start.4 = (bf16[128,2048]{1,0:T(8,128)(2,1)S(1)}, bf16[128,2048]{1,0:T(8,128)(2,1)}, u32[]{:S(2)}) copy-start(bf16[128,2048]{1,0:T(8,128)(2,1)} %copy-done.3) | copy-start | bytes 1572868
Sparse Core Ops, SparseCore 0:
  10.8 47.3 all-gather.2
  60.5 45.4 all-gather.4
  139.8 30.9 reduce-scatter.1

commit v2 on v1

--- a/solution.py
+++ b/solution.py
@@ -119,6 +119,405 @@
         compiler_params=pltpu.CompilerParams(vmem_limit_bytes=58 << 20),
         name="attend",
     )(length, queries, cache_k, cache_v, fresh_k, fresh_v)
+
+
+MESH_ID = pl.DeviceIdType.MESH
+SPLIT = 4
+
+
+def place():
+    group = lax.axis_index("exp")
+    return lax.axis_index("req"), group // 8, (group // 2) % 4, group % 2
+
+
+def ring_peer(part, step, where):
+    plane, row, column, core = where
+    if part == 0:
+        spot = (row + step) % 4
+        return (plane, spot * 8 + column * 2 + core), spot
+    spot = (column + step) % 4
+    return (plane, row * 8 + spot * 2 + core), spot
+
+
+def swap_peer(part, step, where):
+    plane, row, column, core = where
+    side = (core + step) % 2
+    if part == 0:
+        spot = (column + step // 2) % 4
+        return (plane, row * 8 + spot * 2 + side), spot * 2 + side
+    spot = (row + step // 2) % 4
+    return (plane, spot * 8 + column * 2 + side), spot * 2 + side
+
+
+def plane_peer(step, where):
+    plane, row, column, core = where
+    spot = (plane + step) % 4
+    return (spot, row * 8 + column * 2 + core), spot
+
+
+def greet(where):
+    barrier = pltpu.get_barrier_semaphore()
+    peers = [plane_peer(step, where)[0] for step in (1, 2, 3)]
+    peers += [swap_peer(0, step, where)[0] for step in range(1, 8)]
+    peers += [swap_peer(1, step, where)[0] for step in range(2, 8)]
+    for peer in peers:
+        pl.semaphore_signal(barrier, inc=1, device_id=peer, device_id_type=MESH_ID)
+    pl.semaphore_wait(barrier, len(peers))
+
+
+def remote(src, dst, send_sem, recv_sem, peer):
+    return pltpu.make_async_remote_copy(
+        src_ref=src,
+        dst_ref=dst,
+        send_sem=send_sem,
+        recv_sem=recv_sem,
+        device_id=peer,
+        device_id_type=MESH_ID,
+    )
+
+
+def serve_body(
+    rows_ref, map_ref, gate_ref, up_ref, down_ref, made_ref, weigh_ref,
+    tokens, maps, pick, outbox, inbox, w_gate, w_up, w_down, made,
+    z_send, z_recv, b_send, b_recv, c_send, c_recv, m_send, m_recv, n_send, n_recv,
+    local_sem, w_sem, made_sem, weigh_sem,
+):
+    where = place()
+    plane, row, column, core = where
+    at = (row, column)
+    chunk = tokens.shape[-1]
+    loads = [
+        pltpu.make_async_copy(src.at[0], dst, w_sem.at[i])
+        for i, (src, dst) in enumerate(((gate_ref, w_gate), (up_ref, w_up), (down_ref, w_down)))
+    ]
+    for load in loads:
+        load.start()
+    for part in range(2):
+        maps[part, at[part], plane] = map_ref[plane]
+    for q in range(SPLIT):
+        tokens[q, at[q % 2], plane] = rows_ref[:, q * chunk : (q + 1) * chunk]
+    greet(where)
+    sent = []
+
+    def send(copy):
+        copy.start()
+        sent.append(copy)
+
+    for part in range(2):
+        for step in (1, 2, 3):
+            peer, spot = plane_peer(step, where)
+            send(remote(
+                map_ref.at[spot], maps.at[part, at[part], plane],
+                m_send.at[part, step], m_recv.at[part, plane], peer,
+            ))
+    for q in range(SPLIT):
+        for step in (1, 2, 3):
+            peer, spot = plane_peer(step, where)
+            send(remote(
+                rows_ref.at[:, q * chunk : (q + 1) * chunk], tokens.at[q, at[q % 2], plane],
+                z_send.at[q, step], z_recv.at[q, plane], peer,
+            ))
+    for part in range(2):
+        for step in (1, 2, 3):
+            peer, spot = plane_peer(step, where)
+            slot = maps.at[part, at[part], spot]
+            remote(slot, slot, m_send.at[part, step], m_recv.at[part, spot], peer).wait_recv()
+        for step in (1, 2, 3):
+            peer, spot = ring_peer(part, step, where)
+            slot = maps.at[part, at[part]]
+            send(remote(slot, slot, n_send.at[part, step], n_recv.at[part, at[part]], peer))
+    for q in range(SPLIT):
+        part = q % 2
+        for step in (1, 2, 3):
+            peer, spot = plane_peer(step, where)
+            slot = tokens.at[q, at[part], spot]
+            remote(slot, slot, z_send.at[q, step], z_recv.at[q, spot], peer).wait_recv()
+        for step in (1, 2, 3):
+            peer, spot = ring_peer(part, step, where)
+            slot = tokens.at[q, at[part]]
+            send(remote(slot, slot, b_send.at[q, step], b_recv.at[q, at[part]], peer))
+
+    slots = pick.shape[2] // 32
+    group = 4 * slots
+    width = pick.shape[3]
+    r_id = lax.broadcasted_iota(jnp.int32, (group, width), 0)
+    c_id = lax.broadcasted_iota(jnp.int32, (group, width), 1)
+    wanted = jnp.where(
+        r_id // slots == c_id // (width // 4), (r_id % slots + 1).astype(jnp.float32), -1.0
+    )
+    for part in range(2):
+        for step in (1, 2, 3):
+            peer, spot = ring_peer(part, step, where)
+            slot = maps.at[part, spot]
+            remote(slot, slot, n_send.at[part, step], n_recv.at[part, spot], peer).wait_recv()
+
+        def choose(b, carry, part=part):
+            weighed = []
+            for i in range(8):
+                local = row * 8 + i if part == 0 else (i // 2) * 8 + column * 2 + i % 2
+                named = jnp.concatenate(
+                    [maps[part, b, z, pl.ds(local, 1), :] for z in range(4)], axis=1
+                )
+                gates = jnp.concatenate(
+                    [maps[part, b, z, pl.ds(32 + local, 1), :] for z in range(4)], axis=1
+                )
+                hit = wanted == named
+                pick[part, b, i * group : (i + 1) * group, :] = jnp.where(hit, 1.0, 0.0).astype(
+                    jnp.bfloat16
+                )
+                weighed.append(jnp.where(hit, gates, 0.0))
+            made_of = jnp.concatenate(weighed, axis=0)
+            weigh_ref[part, b] = made_of.T.astype(jnp.bfloat16)
+            return carry
+
+        lax.fori_loop(0, 4, choose, 0)
+
+    mine = (column * 2 + core, row * 2 + core)
+    locals_ = []
+    for q in range(SPLIT):
+        part = q % 2
+        cols = pl.ds(q * chunk, chunk)
+        for step in (1, 2, 3):
+            peer, spot = ring_peer(part, step, where)
+            slot = tokens.at[q, spot]
+            remote(slot, slot, b_send.at[q, step], b_recv.at[q, spot], peer).wait_recv()
+
+        def gather(b, carry, q=q, part=part):
+            rows = tokens[q, b].reshape(width, chunk)
+            chosen = jnp.dot(pick[part, b], rows, preferred_element_type=jnp.float32)
+            outbox[q, :, b] = chosen.astype(jnp.bfloat16).reshape(8, group, chunk)
+            return carry
+
+        lax.fori_loop(0, 4, gather, 0)
+
+        def target(row_, column_, core_):
+            if part == 0:
+                return inbox.at[:, column_, core_, :, cols]
+            return inbox.at[row_, :, core_, :, cols]
+
+        for step in range(2, 8):
+            peer, spot = swap_peer(part, step, where)
+            send(remote(
+                outbox.at[q, spot], target(row, column, core),
+                c_send.at[q, step], c_recv.at[q, mine[part]], peer,
+            ))
+        peer, spot = swap_peer(part, 1, where)
+        send(remote(
+            outbox.at[q, spot], target(row, column, core),
+            c_send.at[q, 1], c_recv.at[q, mine[part]], peer,
+        ))
+        own = pltpu.make_async_copy(
+            outbox.at[q, mine[part]], target(row, column, core), local_sem.at[q]
+        )
+        own.start()
+        locals_.append(own)
+    for own in locals_:
+        own.wait()
+    for q in range(SPLIT):
+        part = q % 2
+        cols = pl.ds(q * chunk, chunk)
+        for step in range(1, 8):
+            peer, spot = swap_peer(part, step, where)
+            if part == 0:
+                slot = inbox.at[:, spot // 2, spot % 2, :, cols]
+            else:
+                slot = inbox.at[spot // 2, :, spot % 2, :, cols]
+            remote(
+                outbox.at[q, spot], slot, c_send.at[q, step], c_recv.at[q, spot], peer
+            ).wait_recv()
+    for load in loads:
+        load.wait()
+
+    def expert(r, carry):
+        x = inbox[r].reshape(8 * group, inbox.shape[-1])
+        gate = jnp.dot(x, w_gate[...], preferred_element_type=jnp.float32)
+        up = jnp.dot(x, w_up[...], preferred_element_type=jnp.float32)
+        hidden = (gate / (1.0 + jnp.exp(-gate)) * up).astype(jnp.bfloat16)
+        out = jnp.dot(hidden, w_down[...], preferred_element_type=jnp.float32)
+        made[r] = out.astype(jnp.bfloat16).reshape(made.shape[1:])
+        pltpu.make_async_copy(made.at[r], made_ref.at[r], made_sem.at[r]).start()
+        return carry
+
+    lax.fori_loop(0, 4, expert, 0)
+    for r in range(4):
+        pltpu.make_async_copy(made.at[r], made_ref.at[r], made_sem.at[r]).wait()
+    for copy in sent:
+        copy.wait_send()
+
+
+def serve(rows, maps, w_gate, w_up, w_down, capacity):
+    tokens, width = rows.shape
+    hidden = w_gate.shape[2]
+    chunk = width // SPLIT
+    group = 4 * capacity
+    bf = jnp.bfloat16
+    dma = pltpu.SemaphoreType.DMA
+    vmem = pl.BlockSpec(memory_space=pltpu.VMEM)
+    anywhere = pl.BlockSpec(memory_space=pl.ANY)
+    return pl.pallas_call(
+        serve_body,
+        out_shape=(
+            jax.ShapeDtypeStruct((4, 4, 2, group, width), bf),
+            jax.ShapeDtypeStruct((2, 4, 4 * tokens, 8 * group), bf),
+        ),
+        in_specs=[vmem, vmem, anywhere, anywhere, anywhere],
+        out_specs=(anywhere, vmem),
+        scratch_shapes=[
+            pltpu.VMEM((SPLIT, 4, 4, tokens, chunk), bf),
+            pltpu.VMEM((2, 4, 4) + maps.shape[1:], jnp.float32),
+            pltpu.VMEM((2, 4, 8 * group, 4 * tokens), bf),
+            pltpu.VMEM((SPLIT, 8, 4, group, chunk), bf),
+            pltpu.VMEM((4, 4, 2, group, width), bf),
+            pltpu.VMEM((width, hidden), bf),
+            pltpu.VMEM((width, hidden), bf),
+            pltpu.VMEM((hidden, width), bf),
+            pltpu.VMEM((4, 4, 2, group, width), bf),
+            dma((SPLIT, 4)), dma((SPLIT, 4)),
+            dma((SPLIT, 4)), dma((SPLIT, 4)),
+            dma((SPLIT, 8)), dma((SPLIT, 8)),
+            dma((2, 4)), dma((2, 4)), dma((2, 4)), dma((2, 4)),
+            dma((SPLIT,)), dma((3,)), dma((4,)), dma((1,)),
+        ],
+        compiler_params=pltpu.CompilerParams(
+            collective_id=0, has_side_effects=True, vmem_limit_bytes=62 << 20
+        ),
+        name="serve",
+    )(rows, maps, w_gate, w_up, w_down)
+
+
+def combine_body(
+    made_ref, weigh_ref, base_ref, out_ref,
+    back, share, shares, total, totals,
+    c_send, c_recv, b_send, b_recv, z_send, z_recv, local_sem,
+):
+    where = place()
+    plane, row, column, core = where
+    at = (row, column)
+    mine = (column * 2 + core, row * 2 + core)
+    chunk = total.shape[-1]
+    tokens = base_ref.shape[0]
+    greet(where)
+    sent = []
+
+    def send(copy):
+        copy.start()
+        sent.append(copy)
+
+    for q in range(SPLIT):
+        part = q % 2
+        cols = pl.ds(q * chunk, chunk)
+
+        def source(spot):
+            if part == 0:
+                return made_ref.at[:, spot // 2, spot % 2, :, cols]
+            return made_ref.at[spot // 2, :, spot % 2, :, cols]
+
+        for step in (2, 3, 4, 5, 6, 7, 1):
+            peer, spot = swap_peer(part, step, where)
+            send(remote(
+                source(spot), back.at[q, :, mine[part]],
+                c_send.at[q, step], c_recv.at[q, mine[part]], peer,
+            ))
+        pltpu.make_async_copy(
+            source(mine[part]), back.at[q, :, mine[part]], local_sem.at[q]
+        ).start()
+    for q in range(SPLIT):
+        part = q % 2
+        for step in range(1, 8):
+            peer, spot = swap_peer(part, step, where)
+            slot = back.at[q, :, spot]
+            remote(slot, slot, c_send.at[q, step], c_recv.at[q, spot], peer).wait_recv()
+        slot = back.at[q, :, mine[part]]
+        pltpu.make_async_copy(slot, slot, local_sem.at[q]).wait()
+
+        def weigh(b, carry, q=q, part=part):
+            rows = back[q, b].reshape(weigh_ref.shape[-1], chunk)
+            share[q, b] = jnp.dot(
+                weigh_ref[part, b], rows, preferred_element_type=jnp.float32
+            ).astype(jnp.bfloat16)
+            return carry
+
+        lax.fori_loop(0, 4, weigh, 0)
+        for step in (1, 2, 3):
+            peer, spot = ring_peer(part, step, where)
+            send(remote(
+                share.at[q, spot], shares.at[q, at[part]],
+                b_send.at[q, step], b_recv.at[q, at[part]], peer,
+            ))
+    for q in range(SPLIT):
+        part = q % 2
+        added = share[q, at[part]].astype(jnp.float32)
+        for step in (1, 2, 3):
+            peer, spot = ring_peer(part, step, where)
+            slot = shares.at[q, spot]
+            remote(slot, slot, b_send.at[q, step], b_recv.at[q, spot], peer).wait_recv()
+            added = added + shares[q, spot].astype(jnp.float32)
+        total[q] = added.astype(jnp.bfloat16).reshape(4, tokens, chunk)
+        for step in (1, 2, 3):
+            peer, spot = plane_peer(step, where)
+            send(remote(
+                total.at[q, spot], totals.at[q, plane],
+                z_send.at[q, step], z_recv.at[q, plane], peer,
+            ))
+    for q in range(SPLIT):
+        cols = slice(q * chunk, (q + 1) * chunk)
+        added = total[q, plane].astype(jnp.float32)
+        for step in (1, 2, 3):
+            peer, spot = plane_peer(step, where)
+            slot = totals.at[q, spot]
+            remote(slot, slot, z_send.at[q, step], z_recv.at[q, spot], peer).wait_recv()
+            added = added + totals[q, spot].astype(jnp.float32)
+        out_ref[:, cols] = (base_ref[:, cols].astype(jnp.float32) + added).astype(jnp.bfloat16)
+    for copy in sent:
+        copy.wait_send()
+
+
+def combine(made, weigh, base):
+    tokens, width = base.shape
+    chunk = width // SPLIT
+    group = made.shape[3]
+    bf = jnp.bfloat16
+    dma = pltpu.SemaphoreType.DMA
+    vmem = pl.BlockSpec(memory_space=pltpu.VMEM)
+    return pl.pallas_call(
+        combine_body,
+        out_shape=jax.ShapeDtypeStruct(base.shape, bf),
+        in_specs=[pl.BlockSpec(memory_space=pl.ANY), vmem, vmem],
+        out_specs=vmem,
+        scratch_shapes=[
+            pltpu.VMEM((SPLIT, 4, 8, group, chunk), bf),
+            pltpu.VMEM((SPLIT, 4, 4 * tokens, chunk), bf),
+            pltpu.VMEM((SPLIT, 4, 4 * tokens, chunk), bf),
+            pltpu.VMEM((SPLIT, 4, tokens, chunk), bf),
+            pltpu.VMEM((SPLIT, 4, tokens, chunk), bf),
+            dma((SPLIT, 8)), dma((SPLIT, 8)),
+            dma((SPLIT, 4)), dma((SPLIT, 4)),
+            dma((SPLIT, 4)), dma((SPLIT, 4)), dma((SPLIT,)),
+        ],
+        compiler_params=pltpu.CompilerParams(
+            collective_id=1, has_side_effects=True, vmem_limit_bytes=62 << 20
+        ),
+        name="combine",
+    )(made, weigh, base)
+
+
+def routing_maps(routes, gates, experts, planes):
+    rows = routes.shape[0]
+    ids = routes.T[None, :, :]
+    hit = ids == jnp.arange(experts, dtype=jnp.int32)[:, None, None]
+    named = jnp.sum(hit.astype(jnp.float32), axis=1)
+    weight = jnp.sum(jnp.where(hit, gates.T[None, :, :], 0.0), axis=1)
+    upto = (
+        jnp.arange(rows, dtype=jnp.int32)[:, None] <= jnp.arange(rows, dtype=jnp.int32)[None, :]
+    )
+    order = jnp.dot(
+        named.astype(jnp.bfloat16), upto.astype(jnp.bfloat16), preferred_element_type=jnp.float32
+    )
+    slot = order * named
+    per_plane = experts // planes
+    return jnp.concatenate(
+        [slot.reshape(planes, per_plane, rows), weight.reshape(planes, per_plane, rows)], axis=1
+    )
 
 
 def append(cache, fresh, length):
@@ -187,31 +586,9 @@
     top_k = routes.shape[1]
     experts = groups * lax.axis_size("exp")
     capacity = 3 * top_k * row_count // (2 * experts)
-    flat_ids = routes.reshape(-1)
-    onehot = (flat_ids[:, None] == jnp.arange(experts, dtype=jnp.int32)[None, :]).astype(jnp.int32)
-    slots = jnp.sum((jnp.cumsum(onehot, axis=0) - 1) * onehot, axis=1)
-    target = flat_ids * capacity + slots
-    sources = jnp.arange(row_count * top_k, dtype=jnp.int32) // top_k
-    outgoing = (
-        jnp.zeros((experts * capacity, model_width), jnp.bfloat16).at[target].set(moe_in[sources])
-    )
-    outgoing = outgoing.reshape(experts, capacity, model_width)
-    block_in = lax.all_to_all(outgoing, ("req", "exp"), split_axis=0, concat_axis=0, tiled=True)
-    flat_rows = block_in.reshape(-1, model_width)
-    gate_proj = jnp.dot(flat_rows, w_gate[0], preferred_element_type=jnp.float32)
-    up_proj = jnp.dot(flat_rows, w_up[0], preferred_element_type=jnp.float32)
-    activated = (jax.nn.silu(gate_proj) * up_proj).astype(jnp.bfloat16)
-    produced = jnp.dot(activated, w_down[0], preferred_element_type=jnp.float32).astype(
-        jnp.bfloat16
-    )
-    returned = lax.all_to_all(
-        produced.reshape(block_in.shape), ("req", "exp"), split_axis=0, concat_axis=0, tiled=True
-    )
-    picked = returned.reshape(experts * capacity, model_width)[target].reshape(
-        row_count, top_k, model_width
-    )
-    combined = jnp.sum(picked.astype(jnp.float32) * expert_gates[0][:, :, None], axis=1)
-    result_rows = (after_attn.astype(jnp.float32) + combined).astype(jnp.bfloat16)
+    maps = routing_maps(routes, expert_gates[0], experts, groups)
+    made, weigh = serve(moe_in, maps, w_gate, w_up, w_down, capacity)
+    result_rows = combine(made, weigh, after_attn)
     keys_out = append(cache_keys[0], fresh_keys, length)
     values_out = append(cache_values[0], fresh_values, length)
     return (result_rows[None], keys_out[None], values_out[None])

time: 510 us -> 401 us (0.79)
  Pallas kernels: 50.8 us -> 272 us
  blocking collectives: 103 us -> 0 us
  waiting for transfers between devices: 163 us -> 67.4 us
  local copies, waits for them, and re-layouts: 96.3 us -> 12.7 us
  matrix products: 33.1 us -> 11.7 us
  other arithmetic: 32.6 us -> 19.9 us
  starting transfers between devices: 9.35 us -> 0.12 us
    pallas_call x0 -> x2, Pallas kernels: none -> 222 us  [the longest x1 118 us: serve(): pl.pallas_call(serve_body, out_shape=(jax.ShapeDtypeStruct((4, 4, 2, grou...]
    all_to_all x1 -> x0, blocking collectives: 103 us -> none  [body(): lax.all_to_all(outgoing, ('req', 'exp'), split_axis=0, concat_axis=0, til...]
    all_to_all x1 -> x0, waiting for transfers between devices: 92.2 us -> none  [body(): lax.all_to_all(produced.reshape(block_in.shape), ('req', 'exp'), split_ax...]
    reshape x4 -> x0, local copies, waits for them, and re-layouts: 42.6 us -> none  [the longest x1 10.7 us: body(): flat_rows = block_in.reshape(-1, model_width)]
    scatter x1 -> x0, local copies, waits for them, and re-layouts: 24.1 us -> none  [body(): jnp.zeros((experts * capacity, model_width), jnp.bfloat16).at[target]]
    dot_general x3 -> x1, matrix products: 20.9 us -> 0.14 us  [routing_maps(): jnp.dot(named.astype(jnp.bfloat16), upto.astype(jnp.bfloat16), preferred_...]
    gather x1 -> x0, local copies, waits for them, and re-layouts: 12.4 us -> none  [body(): returned.reshape(experts * capacity, model_width)[target]]
    all_to_all x1 -> x0, starting transfers between devices: 9.23 us -> none  [body(): lax.all_to_all(produced.reshape(block_in.shape), ('req', 'exp'), split_ax...]
  transfers between devices with their start and end apart: 4 -> 3, of which waited for: 3 -> 2; matrix products, arithmetic and copies ran while one was open for 8% -> 8% of each run, Pallas kernels for 10% -> 13%
where the time goes in v2:
time: 401 us; the launch traced here: 398 us
  Pallas kernels  272 us (68%)
  waiting for transfers between devices  67.4 us (17%)
  other arithmetic  19.9 us (5%)
  between operations  14.6 us (4%)
  local copies, waits for them, and re-layouts  12.7 us (3%)
  matrix products  11.7 us (3%)
    pallas_call x1, Pallas kernels, serve(): pl.pallas_call(serve_body, out_shape=(jax.ShapeDtypeStruct((4, 4, 2, grou...  118 us
    pallas_call x1, Pallas kernels, combine(): pl.pallas_call(combine_body, out_shape=jax.ShapeDtypeStruct(base.shape, b...  103 us
    pallas_call x1, Pallas kernels, attend(): pl.pallas_call(functools.partial(attention_body, width ** (-0.5) * math.l...  50.3 us
    all_gather x1, waiting for transfers between devices, body(): lax.all_gather(jnp.concatenate([w_query, w_key, w_value], axis=1), 'exp',...  44.7 us
    reduce_scatter x1, waiting for transfers between devices, body(): lax.psum_scatter(partial_out.astype(jnp.bfloat16), 'req', scatter_dimensi...  22 us
  transfers between devices with their start and end apart: 3, of which 2 were waited for; matrix products, arithmetic and copies ran while one was open for 8% of the time, Pallas kernels for 13%

profile of v2, /device:TPU:26, one launch (start us, length us, event | category | flops | bytes accessed | tf_op | source)
XLA Modules:
  0.0 398.5 jit_solution(5151086697968731314)
XLA Ops:
  7.2 0.0 copy-start.4
  7.2 0.0 copy-start.12
  7.2 0.0 all-gather.3.cloned.1.call-start
  7.2 1.8 pad_maximum_fusion
  9.0 0.0 all-gather.3.cloned.1.call-update
  9.0 0.0 all-gather.5.cloned.1.call-start
  9.1 0.7 all-gather.5.cloned.1.call-update
  9.8 0.0 reduce-scatter.2.cloned.1.call-start
  10.5 2.1 fusion
  12.6 1.0 multiply_cosine_fusion.1
  13.6 44.7 %all-gather.3.cloned.1.call-done = bf16[2048,1280]{1,0:T(8,128)(2,1)} async-done(((bf16[64,1280]{1,0:T(8,128)(2,1)}), bf16[2048,1280]{1,0:T(8,128)(2,1)}) %all-gather.3.cloned.1.call-update) | async-done | bytes 5242896 | tf_op jit(solution)/shard_map/all_gather | solution.py:558
  58.2 0.0 copy-done.12
  58.2 5.4 %fusion.3 = f32[512,1280]{1,0:T(8,128)S(1)} fusion(bf16[2048,1280]{1,0:T(8,128)(2,1)} %all-gather.3.cloned.1.call-done, bf16[1,512,2048]{2,1,0:T(8,128)(2,1)S(1)} %copy-done.4, f32[2048]{0:T(1024)S(1)} %copy-done.12, f32[512]{0:T(512)S(1)} %add_rsqrt_fusion.2), kind=kOutput, calls=%fused_computation.6 | convolution fusion | flops 2688548864 | bytes 9971712 | tf_op jit(solution)/shard_map/dot_general | solution.py:561
  63.7 0.7 slice.47.fv_ref
  64.4 0.8 copy-done.5
  65.2 1.6 slice.29
  66.8 1.9 copy.22
  68.7 0.0 copy-start.10
  68.8 1.9 copy.23
  70.6 1.2 multiply_reduce_fusion.1
  71.9 1.1 multiply_bitcast_fusion
  73.0 1.2 fusion.17
  74.2 0.8 pad_maximum_fusion.1.fk_ref
  75.0 0.3 multiply_reduce_fusion
  75.3 0.7 multiply_multiply_fusion
  76.0 0.8 subtract_convert_fusion
  76.8 1.5 maximum_bitcast_fusion.q_ref
  78.3 50.3 %attend.1 = bf16[512,1024]{1,0:T(8,128)(2,1)} custom-call(s32[1]{0:T(128)} %copy.27.len_ref, bf16[8,512,128]{2,1,0:T(8,128)(2,1)} %maximum_bitcast_fusion.q_ref, bf16[4096,128]{1,0:T(8,128)(2,1)} %bitcast.48, bf16[4096,128]{1,0:T(8,128)(2,1)} %bitcast.50, bf16[512,128]{1,0:T(8,128)(2,1)} %pad_maximum_fusion.1.fk_ref, bf16[512,128]{1,0:T(8,128)(2,1)} %slice.47.fv_ref), custom_call_target="tpu_custom_call" | custom-call | tf_op jit(solution)/shard_map/attend/pallas_call | solution.py:100
  128.6 6.2 %convolution_convert_fusion = bf16[512,2048]{1,0:T(8,128)(2,1)} fusion(bf16[512,1024]{1,0:T(8,128)(2,1)} %attend.1, bf16[1024,2048]{1,0:T(8,128)(2,1)} %all-gather.5.cloned.1.call-done), kind=kOutput, calls=%fused_computation.5 | convolution fusion | flops 2148532224 | bytes 7340032 | tf_op jit(solution)/shard_map/dot_general | solution.py:574
  134.8 0.0 reduce-scatter.2.cloned.1.call-update
  134.9 0.6 copy-done.8
  135.5 0.0 copy-done.9
  135.5 0.3 convert_reduce_fusion
  135.8 0.1 convolution_multiply_fusion
  136.0 0.7 pad_maximum_fusion.2.map_ref
  136.7 0.0 copy-done.2
  136.7 3.9 select_bitcast_fusion
  140.5 1.0 slice_bitcast_fusion
  141.5 1.8 dynamic_update_slice.9
  143.3 0.1 pad_maximum_fusion.3
  143.4 0.5 dynamic_update_slice.8
  143.9 0.0 copy-start.6
  143.9 22.0 %reduce-scatter.2.cloned.1.call-done = bf16[128,2048]{1,0:T(8,128)(2,1)} async-done(((bf16[512,2048]{1,0:T(8,128)(2,1)}), bf16[128,2048]{1,0:T(8,128)(2,1)}) %reduce-scatter.2.cloned.1.call-update) | async-done | bytes 524304 | tf_op jit(solution)/shard_map/reduce_scatter | solution.py:579
  165.9 1.5 fusion.8
  167.4 1.0 fusion.10.rows_ref
  168.4 118.2 %serve.1 = (bf16[4,4,2,48,2048]{4,3,2,1,0:T(8,128)(2,1)}, bf16[2,4,512,384]{3,2,1,0:T(8,128)(2,1)}) custom-call(bf16[128,2048]{1,0:T(8,128)(2,1)} %fusion.10.rows_ref, f32[4,64,128]{2,1,0:T(8,128)} %pad_maximum_fusion.2.map_ref, bf16[1,2048,768]{2,1,0:T(8,128)(2,1)} %gate_ref.1, bf16[1,2048,768]{2,1,0:T(8,128)(2,1)} %up_ref.1, bf16[1,768,2048]{2,1,0:T(8,128)(2,1)} %down_ref.1), custom_call_target="tpu_custom_call" | custom-call | tf_op jit(solution)/shard_map/serve/pallas_call | solution.py:357
  286.6 103.4 %combine.1 = bf16[128,2048]{1,0:T(8,128)(2,1)} custom-call(bf16[4,4,2,48,2048]{4,3,2,1,0:T(8,128)(2,1)} %get-tuple-element.5.made_ref, bf16[2,4,512,384]{3,2,1,0:T(8,128)(2,1)} %get-tuple-element.6.weigh_ref, bf16[128,2048]{1,0:T(8,128)(2,1)} %copy-done.1), custom_call_target="tpu_custom_call" | custom-call | tf_op jit(solution)/shard_map/combine/pallas_call | solution.py:482
  390.0 1.9 copy.28
  (25 shorter events, 0.1 us)
Async XLA Ops:
  7.2 51.1 %copy-start.4 = (bf16[1,512,2048]{2,1,0:T(8,128)(2,1)S(1)}, bf16[1,512,2048]{2,1,0:T(8,128)(2,1)}, u32[]{:S(2)}) copy-start(bf16[1,512,2048]{2,1,0:T(8,128)(2,1)} %param.17) | copy-start | bytes 6291460
  7.2 51.1 %copy-start.12 = (f32[2048]{0:T(1024)S(1)}, f32[2048]{0:T(1024)}, u32[]{:S(2)}) copy-start(f32[2048]{0:T(1024)} %param.21) | copy-start | bytes 24580
  7.2 51.1 %all-gather.3.cloned.1.call-start = ((), (), s32[]{:S(2)}) async-start(), calls=%async_computation.1 | async-start | bytes 5406720 | tf_op jit(solution)/shard_map/all_gather | solution.py:558
  9.0 119.6 %all-gather.5.cloned.1.call-start = ((), (), s32[]{:S(2)}) async-start(), calls=%async_computation.2 | async-start | bytes 4325376 | tf_op jit(solution)/shard_map/all_gather | solution.py:576
  9.8 156.2 %reduce-scatter.2.cloned.1.call-start = ((), (), s32[]{:S(2)}) async-start(), calls=%async_computation.3 | async-start | bytes 2621440 | tf_op jit(solution)/shard_map/reduce_scatter | solution.py:579
  63.7 1.6 copy-start.5
  68.7 3.1 copy-start.10
  70.6 4.7 %copy-start = (f32[512,8,128]{2,0,1:T(8,128)S(1)}, f32[512,8,128]{2,0,1:T(8,128)}, u32[]{:S(2)}) copy-start(f32[512,8,128]{2,0,1:T(8,128)} %copy.23) | copy-start | bytes 6291460
  70.6 4.7 %copy-start.11 = (f32[128]{0:T(128)S(1)}, f32[128]{0:T(128)}, u32[]{:S(2)}) copy-start(f32[128]{0:T(128)} %param.25) | copy-start | bytes 1540
  134.8 0.7 copy-start.8
  134.8 0.7 copy-start.9
  134.8 1.8 copy-start.2
  134.8 1.8 copy-start.3
  140.5 26.9 %copy-start.7 = (f32[2048]{0:T(1024)S(1)}, f32[2048]{0:T(1024)}, u32[]{:S(2)}) copy-start(f32[2048]{0:T(1024)} %param.28) | copy-start | bytes 24580
  143.9 142.7 %copy-start.6 = (bf16[1,4608,128]{2,1,0:T(8,128)(2,1)}, bf16[1,4608,128]{2,1,0:T(8,128)(2,1)S(1)}, u32[]{:S(2)}) copy-start(bf16[1,4608,128]{2,1,0:T(8,128)(2,1)S(1)} %dynamic_update_slice.8) | copy-start | bytes 3538948
  167.4 119.2 %copy-start.1 = (bf16[128,2048]{1,0:T(8,128)(2,1)}, bf16[128,2048]{1,0:T(8,128)(2,1)S(1)}, u32[]{:S(2)}) copy-start(bf16[128,2048]{1,0:T(8,128)(2,1)S(1)} %get-tuple-element.10.base_ref) | copy-start | bytes 1572868
Sparse Core Ops, SparseCore 0:
  10.8 47.3 all-gather.2
  60.5 45.3 all-gather.4
  135.0 30.9 reduce-scatter.1

commit v3 on v2

v3 whole, which is shorter than its diff:
```python
import functools
import math

import jax
import jax.numpy as jnp
from jax import lax
from jax.experimental import pallas as pl
from jax.experimental.pallas import tpu as pltpu
from jax.sharding import PartitionSpec as P

EPS = 1e-06
THETA = 1000000.0


MESH_ID = pl.DeviceIdType.MESH
CHUNKS = ((4, True, 0), (4, True, 1), (4, False, 0), (4, False, 1))
COUNT = len(CHUNKS)
EARLY = COUNT // 2
BACKWARD = (2, 3, 0, 1)


def spans(width):
    unit = width // sum(chunk[0] for chunk in CHUNKS)
    start = 0
    for share, planes_first, part in CHUNKS:
        yield start, share * unit, planes_first, part
        start += share * unit


def place():
    group = lax.axis_index("exp")
    return lax.axis_index("req"), group // 8, (group // 2) % 4, group % 2


def ring_peer(part, step, where):
    plane, row, column, core = where
    if part == 0:
        spot = (row + step) % 4
        return (plane, spot * 8 + column * 2 + core), spot
    spot = (column + step) % 4
    return (plane, row * 8 + spot * 2 + core), spot


def swap_peer(part, step, where):
    plane, row, column, core = where
    side = (core + step) % 2
    if part == 0:
        spot = (column + step // 2) % 4
        return (plane, row * 8 + spot * 2 + side), spot * 2 + side
    spot = (row + step // 2) % 4
    return (plane, spot * 8 + column * 2 + side), spot * 2 + side


def plane_peer(step, where):
    plane, row, column, core = where
    spot = (plane + step) % 4
    return (spot, row * 8 + column * 2 + core), spot


def greet(where):
    barrier = pltpu.get_barrier_semaphore()
    peers = [plane_peer(step, where)[0] for step in (1, 2, 3)]
    peers += [swap_peer(0, step, where)[0] for step in range(1, 8)]
    peers += [swap_peer(1, step, where)[0] for step in range(2, 8)]
    for peer in peers:
        pl.semaphore_signal(barrier, inc=1, device_id=peer, device_id_type=MESH_ID)
    pl.semaphore_wait(barrier, len(peers))


def remote(src, dst, send_sem, recv_sem, peer):
    return pltpu.make_async_remote_copy(
        src_ref=src,
        dst_ref=dst,
        send_sem=send_sem,
        recv_sem=recv_sem,
        device_id=peer,
        device_id_type=MESH_ID,
    )


def hops(planes_first, part, place_at, where):
    along_planes = lambda step: plane_peer(step, where)
    along_ring = lambda step: ring_peer(part, step, where)
    first = (along_planes, where[0]) if planes_first else (along_ring, place_at[part])
    second = (along_ring, place_at[part]) if planes_first else (along_planes, where[0])
    return first, second


def serve_body(
    rows_ref, map_ref, gate_ref, up_ref, down_ref, made_ref, weigh_ref,
    tokens, maps, pick, outbox, inbox, w_gate, w_up, w_down, partial, made,
    f_send, f_recv, b_send, b_recv, c_send, c_recv, m_send, m_recv, n_send, n_recv,
    local_sem, w_sem, made_sem,
):
    where = place()
    plane, row, column, core = where
    at = (row, column)
    chunks = tuple(spans(rows_ref.shape[1]))
    loads = [
        pltpu.make_async_copy(src.at[0], dst, w_sem.at[i])
        for i, (src, dst) in enumerate(((gate_ref, w_gate), (up_ref, w_up), (down_ref, w_down)))
    ]
    for load in loads:
        load.start()
    for part in range(2):
        maps[part, at[part], plane] = map_ref[plane]
    for q, (start, size, planes_first, part) in enumerate(chunks):
        tokens[q][at[part], plane] = rows_ref[:, start : start + size]
    greet(where)
    sent = []

    def send(copy):
        copy.start()
        sent.append(copy)

    for part in range(2):
        for step in (1, 2, 3):
            peer, spot = plane_peer(step, where)
            send(remote(
                map_ref.at[spot], maps.at[part, at[part], plane],
                m_send.at[part, step], m_recv.at[part, plane], peer,
            ))
    for q, (start, size, planes_first, part) in enumerate(chunks):
        (first, here), _ = hops(planes_first, part, at, where)
        for step in (1, 2, 3):
            peer, spot = first(step)
            send(remote(
                rows_ref.at[:, start : start + size], tokens[q].at[at[part], plane],
                f_send.at[q, step], f_recv.at[q, here], peer,
            ))
    for part in range(2):
        for step in (1, 2, 3):
            peer, spot = plane_peer(step, where)
            slot = maps.at[part, at[part], spot]
            remote(slot, slot, m_send.at[part, step], m_recv.at[part, spot], peer).wait_recv()
        for step in (1, 2, 3):
            peer, spot = ring_peer(part, step, where)
            slot = maps.at[part, at[part]]
            send(remote(slot, slot, n_send.at[part, step], n_recv.at[part, at[part]], peer))
    for q, (start, size, planes_first, part) in enumerate(chunks):
        (first, _), (second, here) = hops(planes_first, part, at, where)
        for step in (1, 2, 3):
            peer, spot = first(step)
            slot = tokens[q].at[at[part], spot] if planes_first else tokens[q].at[spot, plane]
            remote(slot, slot, f_send.at[q, step], f_recv.at[q, spot], peer).wait_recv()
        for step in (1, 2, 3):
            peer, spot = second(step)
            slot = tokens[q].at[at[part]] if planes_first else tokens[q].at[:, plane]
            send(remote(slot, slot, b_send.at[q, step], b_recv.at[q, here], peer))

    slots = pick.shape[2] // 32
    group = 4 * slots
    width = pick.shape[3]
    r_id = lax.broadcasted_iota(jnp.int32, (group, width), 0)
    c_id = lax.broadcasted_iota(jnp.int32, (group, width), 1)
    wanted = jnp.where(
        r_id // slots == c_id // (width // 4), (r_id % slots + 1).astype(jnp.float32), -1.0
    )
    for part in range(2):
        for step in (1, 2, 3):
            peer, spot = ring_peer(part, step, where)
            slot = maps.at[part, spot]
            remote(slot, slot, n_send.at[part, step], n_recv.at[part, spot], peer).wait_recv()

        def choose(b, carry, part=part):
            weighed = []
            for i in range(8):
                local = row * 8 + i if part == 0 else (i // 2) * 8 + column * 2 + i % 2
                named = jnp.concatenate(
                    [maps[part, b, z, pl.ds(local, 1), :] for z in range(4)], axis=1
                )
                gates = jnp.concatenate(
                    [maps[part, b, z, pl.ds(32 + local, 1), :] for z in range(4)], axis=1
                )
                hit = wanted == named
                pick[part, b, i * group : (i + 1) * group, :] = jnp.where(hit, 1.0, 0.0).astype(
                    jnp.bfloat16
                )
                weighed.append(jnp.where(hit, gates, 0.0))
            made_of = jnp.concatenate(weighed, axis=0)
            weigh_ref[part, b] = made_of.T.astype(jnp.bfloat16)
            return carry

        lax.fori_loop(0, 4, choose, 0)

    mine = (column * 2 + core, row * 2 + core)
    owns = []
    for q, (start, size, planes_first, part) in enumerate(chunks):
        _, (second, _) = hops(planes_first, part, at, where)
        for step in (1, 2, 3):
            peer, spot = second(step)
            slot = tokens[q].at[spot] if planes_first else tokens[q].at[:, spot]
            remote(slot, slot, b_send.at[q, step], b_recv.at[q, spot], peer).wait_recv()

        def gather(b, carry, q=q, part=part, size=size):
            rows = tokens[q][b].reshape(width, size)
            chosen = jnp.dot(pick[part, b], rows, preferred_element_type=jnp.float32)
            outbox[q][:, b] = chosen.astype(jnp.bfloat16).reshape(8, group, size)
            return carry

        lax.fori_loop(0, 4, gather, 0)
        cols = pl.ds(start, size)
        target = inbox.at[:, column, core, :, cols] if part == 0 else inbox.at[row, :, core, :, cols]
        for step in (2, 3, 4, 5, 6, 7, 1):
            peer, spot = swap_peer(part, step, where)
            send(remote(
                outbox[q].at[spot], target, c_send.at[q, step], c_recv.at[q, mine[part]], peer
            ))
        own = pltpu.make_async_copy(outbox[q].at[mine[part]], target, local_sem.at[q])
        own.start()
        owns.append(own)

    def arrive(which):
        for q in which:
            start, size, planes_first, part = chunks[q]
            cols = pl.ds(start, size)
            owns[q].wait()
            for step in range(1, 8):
                peer, spot = swap_peer(part, step, where)
                if part == 0:
                    slot = inbox.at[:, spot // 2, spot % 2, :, cols]
                else:
                    slot = inbox.at[spot // 2, :, spot % 2, :, cols]
                remote(
                    outbox[q].at[spot], slot, c_send.at[q, step], c_recv.at[q, spot], peer
                ).wait_recv()

    cut = chunks[EARLY][0]
    hidden_width = w_gate.shape[1]
    arrive(range(EARLY))
    for load in loads:
        load.wait()

    def begin(r, carry):
        x = inbox[r, :, :, :, 0:cut].reshape(8 * group, cut)
        partial[r, :, 0:hidden_width] = jnp.dot(
            x, w_gate[0:cut, :], preferred_element_type=jnp.float32
        )
        partial[r, :, hidden_width:] = jnp.dot(
            x, w_up[0:cut, :], preferred_element_type=jnp.float32
        )
        return carry

    lax.fori_loop(0, 4, begin, 0)
    arrive(range(EARLY, COUNT))

    def expert(r, carry):
        x = inbox[r, :, :, :, cut:].reshape(8 * group, inbox.shape[-1] - cut)
        gate = partial[r, :, 0:hidden_width] + jnp.dot(
            x, w_gate[cut:, :], preferred_element_type=jnp.float32
        )
        up = partial[r, :, hidden_width:] + jnp.dot(
            x, w_up[cut:, :], preferred_element_type=jnp.float32
        )
        hidden = (gate / (1.0 + jnp.exp(-gate)) * up).astype(jnp.bfloat16)
        out = jnp.dot(hidden, w_down[...], preferred_element_type=jnp.float32)

        @pl.when(r >= 2)
        def _():
            pltpu.make_async_copy(made.at[r % 2], made_ref.at[r - 2], made_sem.at[r % 2]).wait()

        made[r % 2] = out.astype(jnp.bfloat16).reshape(made.shape[1:])
        pltpu.make_async_copy(made.at[r % 2], made_ref.at[r], made_sem.at[r % 2]).start()
        return carry

    lax.fori_loop(0, 4, expert, 0)
    for r in (2, 3):
        pltpu.make_async_copy(made.at[r % 2], made_ref.at[r], made_sem.at[r % 2]).wait()
    for copy in sent:
        copy.wait_send()


def serve(rows, maps, w_gate, w_up, w_down, capacity):
    tokens, width = rows.shape
    hidden = w_gate.shape[2]
    sizes = [size for _, size, _, _ in spans(width)]
    group = 4 * capacity
    bf = jnp.bfloat16
    dma = pltpu.SemaphoreType.DMA
    vmem = pl.BlockSpec(memory_space=pltpu.VMEM)
    anywhere = pl.BlockSpec(memory_space=pl.ANY)
    return pl.pallas_call(
        serve_body,
        out_shape=(
            jax.ShapeDtypeStruct((4, 4, 2, group, width), bf),
            jax.ShapeDtypeStruct((2, 4, 4 * tokens, 8 * group), bf),
        ),
        in_specs=[vmem, vmem, anywhere, anywhere, anywhere],
        out_specs=(anywhere, vmem),
        scratch_shapes=[
            [pltpu.VMEM((4, 4, tokens, size), bf) for size in sizes],
            pltpu.VMEM((2, 4, 4) + maps.shape[1:], jnp.float32),
            pltpu.VMEM((2, 4, 8 * group, 4 * tokens), bf),
            [pltpu.VMEM((8, 4, group, size), bf) for size in sizes],
            pltpu.VMEM((4, 4, 2, group, width), bf),
            pltpu.VMEM((width, hidden), bf),
            pltpu.VMEM((width, hidden), bf),
            pltpu.VMEM((hidden, width), bf),
            pltpu.VMEM((4, 8 * group, 2 * hidden), jnp.float32),
            pltpu.VMEM((2, 4, 2, group, width), bf),
            dma((COUNT, 4)), dma((COUNT, 4)),
            dma((COUNT, 4)), dma((COUNT, 4)),
            dma((COUNT, 8)), dma((COUNT, 8)),
            dma((2, 4)), dma((2, 4)), dma((2, 4)), dma((2, 4)),
            dma((COUNT,)), dma((3,)), dma((2,)),
        ],
        compiler_params=pltpu.CompilerParams(
            collective_id=0, has_side_effects=True, vmem_limit_bytes=63 << 20
        ),
        name="serve",
    )(rows, maps, w_gate, w_up, w_down)


def combine_body(
    made_ref, weigh_ref, base_ref, out_ref,
    back, share, shares, total, totals,
    c_send, c_recv, b_send, b_recv, f_send, f_recv, local_sem,
):
    where = place()
    plane, row, column, core = where
    at = (row, column)
    mine = (column * 2 + core, row * 2 + core)
    tokens = base_ref.shape[0]
    forward = tuple(spans(base_ref.shape[1]))
    chunks = tuple((q, forward[q]) for q in BACKWARD)
    greet(where)
    sent = []

    def send(copy):
        copy.start()
        sent.append(copy)

    for q, (start, size, planes_first, part) in chunks:
        cols = pl.ds(start, size)

        def source(spot):
            if part == 0:
                return made_ref.at[:, spot // 2, spot % 2, :, cols]
            return made_ref.at[spot // 2, :, spot % 2, :, cols]

        for step in (2, 3, 4, 5, 6, 7, 1):
            peer, spot = swap_peer(part, step, where)
            send(remote(
                source(spot), back[q].at[:, mine[part]],
                c_send.at[q, step], c_recv.at[q, mine[part]], peer,
            ))
        pltpu.make_async_copy(
            source(mine[part]), back[q].at[:, mine[part]], local_sem.at[q]
        ).start()
    for q, (start, size, planes_first, part) in chunks:
        for step in range(1, 8):
            peer, spot = swap_peer(part, step, where)
            slot = back[q].at[:, spot]
            remote(slot, slot, c_send.at[q, step], c_recv.at[q, spot], peer).wait_recv()
        slot = back[q].at[:, mine[part]]
        pltpu.make_async_copy(slot, slot, local_sem.at[q]).wait()

        def weigh(b, carry, q=q, part=part, size=size):
            rows = back[q][b].reshape(weigh_ref.shape[-1], size)
            summed = jnp.dot(weigh_ref[part, b], rows, preferred_element_type=jnp.float32)
            share[q][b] = summed.astype(jnp.bfloat16).reshape(4, tokens, size)
            return carry

        lax.fori_loop(0, 4, weigh, 0)
        _, (second, here) = hops(planes_first, part, at, where)
        for step in (1, 2, 3):
            peer, spot = second(step)
            slot = share[q].at[spot] if planes_first else share[q].at[:, spot]
            send(remote(
                slot, shares[q].at[here], b_send.at[q, step], b_recv.at[q, here], peer
            ))
    for q, (start, size, planes_first, part) in chunks:
        (first, near), (second, here) = hops(planes_first, part, at, where)
        added = share[q][here] if planes_first else share[q][:, here]
        added = added.astype(jnp.float32)
        for step in (1, 2, 3):
            peer, spot = second(step)
            slot = shares[q].at[spot]
            remote(slot, slot, b_send.at[q, step], b_recv.at[q, spot], peer).wait_recv()
            added = added + shares[q][spot].astype(jnp.float32)
        total[q][...] = added.astype(jnp.bfloat16)
        for step in (1, 2, 3):
            peer, spot = first(step)
            send(remote(
                total[q].at[spot], totals[q].at[near],
                f_send.at[q, step], f_recv.at[q, near], peer,
            ))
    for q, (start, size, planes_first, part) in chunks:
        (first, near), _ = hops(planes_first, part, at, where)
        cols = slice(start, start + size)
        added = total[q][near].astype(jnp.float32)
        for step in (1, 2, 3):
            peer, spot = first(step)
            slot = totals[q].at[spot]
            remote(slot, slot, f_send.at[q, step], f_recv.at[q, spot], peer).wait_recv()
            added = added + totals[q][spot].astype(jnp.float32)
        out_ref[:, cols] = (base_ref[:, cols].astype(jnp.float32) + added).astype(jnp.bfloat16)
    for copy in sent:
        copy.wait_send()


def combine(made, weigh, base):
    tokens, width = base.shape
    sizes = [size for _, size, _, _ in spans(width)]
    group = made.shape[3]
    bf = jnp.bfloat16
    dma = pltpu.SemaphoreType.DMA
    vmem = pl.BlockSpec(memory_space=pltpu.VMEM)
    return pl.pallas_call(
        combine_body,
        out_shape=jax.ShapeDtypeStruct(base.shape, bf),
        in_specs=[pl.BlockSpec(memory_space=pl.ANY), vmem, vmem],
        out_specs=vmem,
        scratch_shapes=[
            [pltpu.VMEM((4, 8, group, size), bf) for size in sizes],
            [pltpu.VMEM((4, 4, tokens, size), bf) for size in sizes],
            [pltpu.VMEM((4, 4, tokens, size), bf) for size in sizes],
            [pltpu.VMEM((4, tokens, size), bf) for size in sizes],
            [pltpu.VMEM((4, tokens, size), bf) for size in sizes],
            dma((COUNT, 8)), dma((COUNT, 8)),
            dma((COUNT, 4)), dma((COUNT, 4)),
            dma((COUNT, 4)), dma((COUNT, 4)), dma((COUNT,)),
        ],
        compiler_params=pltpu.CompilerParams(
            collective_id=1, has_side_effects=True, vmem_limit_bytes=62 << 20
        ),
        name="combine",
    )(made, weigh, base)


def routing_maps(routes, gates, experts, planes):
    rows = routes.shape[0]
    ids = routes.T[None, :, :]
    hit = ids == jnp.arange(experts, dtype=jnp.int32)[:, None, None]
    named = jnp.sum(hit.astype(jnp.float32), axis=1)
    weight = jnp.sum(jnp.where(hit, gates.T[None, :, :], 0.0), axis=1)
    upto = (
        jnp.arange(rows, dtype=jnp.int32)[:, None] <= jnp.arange(rows, dtype=jnp.int32)[None, :]
    )
    order = jnp.dot(
        named.astype(jnp.bfloat16), upto.astype(jnp.bfloat16), preferred_element_type=jnp.float32
    )
    slot = order * named
    per_plane = experts // planes
    return jnp.concatenate(
        [slot.reshape(planes, per_plane, rows), weight.reshape(planes, per_plane, rows)], axis=1
    )


def front_body(
    exp_scale, length_ref, tokens_ref, gain_ref, wq_ref, wk_ref, wv_ref, cos_ref, sin_ref,
    q_gain_ref, k_gain_ref, ck_ref, cv_ref, wo_ref, moe_gain_ref,
    after_ref, moe_ref, fk_ref, fv_ref,
    weights, w_out, normed, proj, queries, kaug, vaug, attended, share, shares,
    s_send, s_recv, t_send, t_recv, x_send, x_recv, z_send, z_recv, cache_sem,
):
    where = place()
    plane, row, column, core = where
    stretch_len = tokens_ref.shape[0]
    width = q_gain_ref.shape[1]
    heads = queries.shape[0]
    cached = ck_ref.shape[1]
    fresh = fk_ref.shape[0]
    block = stretch_len // 4
    caches = [
        pltpu.make_async_copy(src.at[0], dst.at[0:cached, 0:width], cache_sem.at[i])
        for i, (src, dst) in enumerate(((ck_ref, kaug), (cv_ref, vaug)))
    ]
    for copy in caches:
        copy.start()
    q_cols = wq_ref.shape[1]
    k_cols = wk_ref.shape[1]
    weights[row, column, core, :, 0:q_cols] = wq_ref[...]
    weights[row, column, core, :, q_cols : q_cols + k_cols] = wk_ref[...]
    weights[row, column, core, :, q_cols + k_cols :] = wv_ref[...]
    w_out[row, column, core] = wo_ref[...]
    greet(where)
    sent = []

    def send(copy):
        copy.start()
        sent.append(copy)

    arrays = (weights, w_out)

    def half(array, part):
        middle = array.shape[-1] // 2
        return slice(0, middle) if part == 0 else slice(middle, 2 * middle)

    def near(n, part, spot_row, spot_column, side):
        return arrays[n].at[spot_row, spot_column, side, :, half(arrays[n], part)]

    def line(n, part, spot):
        if part == 0:
            return arrays[n].at[:, spot, core, :, half(arrays[n], part)]
        return arrays[n].at[spot, :, core, :, half(arrays[n], part)]

    at = (row, column)
    across = (column, row)
    for n in range(2):
        for part in range(2):
            for step in (1, 2, 3):
                peer, spot = ring_peer(part, step, where)
                slot = near(n, part, row, column, core)
                send(remote(
                    slot, slot, s_send.at[n, part, step], s_recv.at[n, part, at[part]], peer
                ))

    def second_stage(n):
        for part in range(2):
            for step in (1, 2, 3):
                peer, spot = ring_peer(part, step, where)
                slot = near(n, part, spot, column, core) if part == 0 else near(
                    n, part, row, spot, core
                )
                remote(
                    slot, slot, s_send.at[n, part, step], s_recv.at[n, part, spot], peer
                ).wait_recv()
            for step in (1, 2, 3):
                peer, spot = ring_peer(1 - part, step, where)
                slot = line(n, part, across[part])
                send(remote(
                    slot, slot, t_send.at[n, part, step], t_recv.at[n, part, across[part]], peer
                ))

    def hand_over(n):
        for part in range(2):
            for step in (1, 2, 3):
                peer, spot = ring_peer(1 - part, step, where)
                slot = line(n, part, spot)
                remote(
                    slot, slot, t_send.at[n, part, step], t_recv.at[n, part, spot], peer
                ).wait_recv()
            peer, _ = swap_peer(0, 1, where)
            slot = arrays[n].at[:, :, core, :, half(arrays[n], part)]
            pair(n, part).start()

    def pair(n, part):
        peer, _ = swap_peer(0, 1, where)
        slot = arrays[n].at[:, :, core, :, half(arrays[n], part)]
        return remote(slot, slot, x_send.at[n, part], x_recv.at[n, part], peer)

    def handed(n):
        for part in range(2):
            peer, _ = swap_peer(0, 1, where)
            slot = arrays[n].at[:, :, 1 - core, :, half(arrays[n], part)]
            remote(slot, slot, x_send.at[n, part], x_recv.at[n, part], peer).wait_recv()

    def normalize(i, carry):
        rows = pl.ds(i * block, block)
        values = tokens_ref[rows, :].astype(jnp.float32)
        factor = lax.rsqrt(jnp.mean(values * values, axis=-1, keepdims=True) + EPS)
        normed[rows, :] = (values * factor * gain_ref[...]).astype(jnp.bfloat16)
        return carry

    lax.fori_loop(0, 4, normalize, 0)
    second_stage(0)
    span = cached + fresh
    position = lax.broadcasted_iota(jnp.int32, (span, width), 0)
    lane = lax.broadcasted_iota(jnp.int32, (span, width), 1)
    hidden = (lane == 0) & (position >= length_ref[0]) & (position < cached)
    kaug[:, width:] = jnp.where(hidden, -1e30, 0.0).astype(jnp.bfloat16)
    vaug[:, width:] = jnp.ones((span, width), jnp.bfloat16)
    hand_over(0)
    second_stage(1)
    handed(0)

    def project(i, carry):
        rows = pl.ds(i * block, block)
        flat = weights[...].reshape(normed.shape[1], weights.shape[-1])
        proj[rows, :] = jnp.dot(normed[rows, :], flat, preferred_element_type=jnp.float32)
        return carry

    lax.fori_loop(0, 4, project, 0)

    def turned(values, gain):
        factor = lax.rsqrt(jnp.mean(values * values, axis=-1, keepdims=True) + EPS)
        values = values * factor * gain
        swapped = pltpu.roll(values, width // 2, 1)
        return (values * cos_ref[...] + swapped * sin_ref[...]).astype(jnp.bfloat16)

    for head in range(heads):
        queries[head] = turned(proj[:, head * width : (head + 1) * width], q_gain_ref[...])
    new_keys = turned(proj[:, q_cols : q_cols + k_cols], k_gain_ref[...])
    new_values = proj[:, q_cols + k_cols :].astype(jnp.bfloat16)
    fk_ref[...] = new_keys
    fv_ref[...] = new_values
    for copy in caches:
        copy.wait()
    kaug[cached:, 0:width] = new_keys
    vaug[cached:, 0:width] = new_values

    dims = (((1,), (1,)), ((), ()))
    count = heads * block

    def attend(spot):
        own = queries[:, pl.ds(spot * block, block), :].reshape(count, width)
        widened = jnp.concatenate([own, jnp.ones((count, width), jnp.bfloat16)], axis=1)
        old = lax.dot_general(widened, kaug[0:cached, :], dims, preferred_element_type=jnp.float32)
        new = lax.dot_general(
            own, kaug[cached:, 0:width], dims, preferred_element_type=jnp.float32
        )
        token = lax.broadcasted_iota(jnp.int32, (count, fresh), 0) % block + spot * block
        new = jnp.where(lax.broadcasted_iota(jnp.int32, (count, fresh), 1) <= token, new, -1e30)
        peak = jnp.maximum(
            jnp.max(old, axis=1, keepdims=True), jnp.max(new, axis=1, keepdims=True)
        )
        old = jnp.exp2((old - peak) * exp_scale).astype(jnp.bfloat16)
        new = jnp.exp2((new - peak) * exp_scale).astype(jnp.bfloat16)
        mixed = jnp.dot(old, vaug[0:cached, :], preferred_element_type=jnp.float32) + jnp.dot(
            new, vaug[cached:, :], preferred_element_type=jnp.float32
        )
        mixed = (mixed[:, :width] / mixed[:, width:]).astype(jnp.bfloat16)
        for head in range(heads):
            attended[spot, :, head * width : (head + 1) * width] = mixed[
                head * block : (head + 1) * block
            ]

    def project_out(spot):
        flat = w_out[...].reshape(attended.shape[2], w_out.shape[-1])
        return jnp.dot(attended[spot], flat, preferred_element_type=jnp.float32)

    def give(i):
        spot = (plane + 1 + i) % 4
        share[spot] = project_out(spot).astype(jnp.bfloat16)
        remote(
            share.at[spot], shares.at[plane], z_send.at[spot], z_recv.at[plane],
            (spot, row * 8 + column * 2 + core),
        ).start()

    def turn(i, carry):
        attend((plane + 1 + i) % 4)

        @pl.when(i == 0)
        def _():
            hand_over(1)

        @pl.when(i == 1)
        def _():
            handed(1)
            give(0)

        @pl.when((i > 0) & (i < 3))
        def _():
            give(i)

        return carry

    lax.fori_loop(0, 4, turn, 0)
    added = project_out(plane)
    for step in (1, 2, 3):
        peer, spot = plane_peer(step, where)
        remote(
            share.at[spot], shares.at[spot], z_send.at[spot], z_recv.at[spot], peer
        ).wait_recv()
        added = added + shares[spot].astype(jnp.float32)
    resident = tokens_ref[pl.ds(pl.multiple_of(plane * block, block), block), :]
    after = (resident.astype(jnp.float32) + added).astype(jnp.bfloat16)
    after_ref[...] = after
    values = after.astype(jnp.float32)
    factor = lax.rsqrt(jnp.mean(values * values, axis=-1, keepdims=True) + EPS)
    moe_ref[...] = (values * factor * moe_gain_ref[...]).astype(jnp.bfloat16)
    for copy in sent:
        copy.wait_send()
    for n in range(2):
        for part in range(2):
            pair(n, part).wait_send()
    for step in (1, 2, 3):
        peer, spot = plane_peer(step, where)
        remote(
            share.at[spot], shares.at[spot], z_send.at[spot], z_recv.at[spot], peer
        ).wait_send()


def front(
    length, tokens, attn_gain, w_query, w_key, w_value, cosine, sine, q_gain, k_gain,
    cache_keys, cache_values, w_out, moe_gain,
):
    stretch_len, model_width = tokens.shape
    width = q_gain.shape[0]
    heads = w_query.shape[1] // width
    columns = w_query.shape[1] + w_key.shape[1] + w_value.shape[1]
    span = cache_keys.shape[1] + stretch_len
    block = stretch_len // 4
    bf = jnp.bfloat16
    dma = pltpu.SemaphoreType.DMA
    vmem = pl.BlockSpec(memory_space=pltpu.VMEM)
    anywhere = pl.BlockSpec(memory_space=pl.ANY)
    return pl.pallas_call(
        functools.partial(front_body, width ** -0.5 * math.log2(math.e)),
        out_shape=(
            jax.ShapeDtypeStruct((block, model_width), bf),
            jax.ShapeDtypeStruct((block, model_width), bf),
            jax.ShapeDtypeStruct((stretch_len, width), bf),
            jax.ShapeDtypeStruct((stretch_len, width), bf),
        ),
        in_specs=[pl.BlockSpec(memory_space=pltpu.SMEM)] + [vmem] * 9 + [anywhere] * 2 + [vmem] * 2,
        out_specs=(vmem,) * 4,
        scratch_shapes=[
            pltpu.VMEM((4, 4, 2, w_query.shape[0], columns), bf),
            pltpu.VMEM((4, 4, 2, w_out.shape[0], model_width), bf),
            pltpu.VMEM((stretch_len, model_width), bf),
            pltpu.VMEM((stretch_len, columns), jnp.float32),
            pltpu.VMEM((heads, stretch_len, width), bf),
            pltpu.VMEM((span, 2 * width), bf),
            pltpu.VMEM((span, 2 * width), bf),
            pltpu.VMEM((4, block, heads * width), bf),
            pltpu.VMEM((4, block, model_width), bf),
            pltpu.VMEM((4, block, model_width), bf),
            dma((2, 2, 4)), dma((2, 2, 4)), dma((2, 2, 4)), dma((2, 2, 4)),
            dma((2, 2)), dma((2, 2)), dma((4,)), dma((4,)), dma((2,)),
        ],
        compiler_params=pltpu.CompilerParams(
            collective_id=2, has_side_effects=True, vmem_limit_bytes=63 << 20
        ),
        name="front",
    )(
        length, tokens, attn_gain[None], w_query, w_key, w_value, cosine, sine,
        q_gain[None], k_gain[None], cache_keys, cache_values, w_out, moe_gain[None],
    )


def turning(length, stretch_len, width):
    half_dim = width // 2
    frequency = THETA ** (-jnp.arange(half_dim, dtype=jnp.float32) * 2.0 / width)
    positions = length + jnp.arange(stretch_len, dtype=jnp.int32)
    angles = positions.astype(jnp.float32)[:, None] * frequency[None, :]
    cosine, sine = jnp.cos(angles), jnp.sin(angles)
    return jnp.concatenate([cosine, cosine], axis=1), jnp.concatenate([-sine, sine], axis=1)


def append(cache, fresh, length):
    span = cache.shape[0] + fresh.shape[0]
    padded = jnp.concatenate([cache, jnp.zeros_like(fresh)], axis=0)
    kept_rows = jnp.where(
        (jnp.arange(span, dtype=jnp.int32) < length)[:, None], padded, jnp.zeros_like(padded)
    )
    return lax.dynamic_update_slice(kept_rows, fresh, (length, jnp.zeros((), jnp.int32)))


def body(
    hidden_in,
    cache_keys,
    cache_values,
    cache_len,
    attn_gain,
    w_query,
    w_key,
    w_value,
    q_gain,
    k_gain,
    w_out,
    moe_gain,
    expert_ids,
    expert_gates,
    w_gate,
    w_up,
    w_down,
):
    tokens = hidden_in[0]
    stretch_len = tokens.shape[0]
    length = cache_len[0]
    groups = lax.axis_size("req")
    row_count = stretch_len // groups
    cosine, sine = turning(length, stretch_len, q_gain.shape[0])
    after_attn, moe_in, fresh_keys, fresh_values = front(
        cache_len, tokens, attn_gain, w_query, w_key, w_value, cosine, sine, q_gain, k_gain,
        cache_keys, cache_values, w_out, moe_gain,
    )
    routes = expert_ids[0]
    top_k = routes.shape[1]
    experts = groups * lax.axis_size("exp")
    capacity = 3 * top_k * row_count // (2 * experts)
    maps = routing_maps(routes, expert_gates[0], experts, groups)
    made, weigh = serve(moe_in, maps, w_gate, w_up, w_down, capacity)
    result_rows = combine(made, weigh, after_attn)
    keys_out = append(cache_keys[0], fresh_keys, length)
    values_out = append(cache_values[0], fresh_values, length)
    return (result_rows[None], keys_out[None], values_out[None])


def solution(mesh):
    placed = (
        P("exp", None, None),
        P("exp", None, "req"),
        P("exp", None, "req"),
        P("exp"),
        P(),
        P("exp", "req"),
        P("exp", "req"),
        P("exp", "req"),
        P(),
        P(),
        P(("req", "exp"), None),
        P(),
        P("exp", "req", None),
        P("exp", "req", None),
        P(("req", "exp"), None, None),
        P(("req", "exp"), None, None),
        P(("req", "exp"), None, None),
    )
    return jax.shard_map(
        body,
        mesh=mesh,
        in_specs=placed,
        out_specs=(P("exp", "req", None), P("exp", None, "req"), P("exp", None, "req")),
        check_vma=False,
    )
```

time: 401 us -> 302 us (0.75)
  waiting for transfers between devices: 67.4 us -> 0 us
  between operations: 14.6 us -> 1.4 us
  Pallas kernels: 272 us -> 284 us
  other arithmetic: 19.9 us -> 8.05 us
  matrix products: 11.7 us -> 0.14 us
  local copies, waits for them, and re-layouts: 12.7 us -> 4.37 us
    all_gather x2 -> x0, waiting for transfers between devices: 44.7 us -> none  [the longest x1 44.7 us: body(): lax.all_gather(jnp.concatenate([w_query, w_key, w_value], axis=1), 'exp',...]
    pallas_call x1, Pallas kernels: 50.3 us -> 91.4 us  [front(): pl.pallas_call(functools.partial(front_body, width ** (-0.5) * math.log2(...]
    reduce_scatter x1 -> x0, waiting for transfers between devices: 22 us -> none  [body(): lax.psum_scatter(partial_out.astype(jnp.bfloat16), 'req', scatter_dimensi...]
    pallas_call x1, Pallas kernels: 118 us -> 102 us  [serve(): pl.pallas_call(serve_body, out_shape=(jax.ShapeDtypeStruct((4, 4, 2, grou...]
    pallas_call x1, Pallas kernels: 103 us -> 90 us  [combine(): pl.pallas_call(combine_body, out_shape=jax.ShapeDtypeStruct(base.shape, b...]
    dot_general x2 -> x0, matrix products: 11.6 us -> none  [the longest x1 6.19 us: body(): jnp.dot(block_in, lax.all_gather(w_out, 'exp', axis=0, tiled=True), prefe...]
    reduce_sum x4 -> x0, other arithmetic: 5.06 us -> none  [rms_norm(): factor = lax.rsqrt(jnp.mean(values * values, axis=-1, keepdims=True) + EPS)]
    slice x3 -> x0, local copies, waits for them, and re-layouts: 4.25 us -> none  [the longest x2 3.52 us: body(): query_proj = proj[:, :widths[0]]]
  transfers between devices with their start and end apart: 3 -> 0, of which waited for: 2 -> 0; matrix products, arithmetic and copies ran while one was open for 8% -> 0% of each run, Pallas kernels for 13% -> 0%
where the time goes in v3:
time: 302 us; the launch traced here: 298 us
  Pallas kernels  284 us (94%)
  other arithmetic  8.05 us (3%)
  local copies, waits for them, and re-layouts  4.37 us (1%)
    pallas_call x1, Pallas kernels, serve(): pl.pallas_call(serve_body, out_shape=(jax.ShapeDtypeStruct((4, 4, 2, grou...  102 us
    pallas_call x1, Pallas kernels, front(): pl.pallas_call(functools.partial(front_body, width ** (-0.5) * math.log2(...  91.4 us
    pallas_call x1, Pallas kernels, combine(): pl.pallas_call(combine_body, out_shape=jax.ShapeDtypeStruct(base.shape, b...  90 us

profile of v3, /device:TPU:26, one launch (start us, length us, event | category | flops | bytes accessed | tf_op | source)
XLA Modules:
  0.0 297.8 jit_solution(17289311813196089948)
XLA Ops:
  1.3 1.0 fusion
  2.3 1.0 pad_maximum_fusion
  3.3 0.0 copy-start.4
  3.3 0.0 copy-start.5
  3.3 91.4 %front.1 = (bf16[128,2048]{1,0:T(8,128)(2,1)}, bf16[128,2048]{1,0:T(8,128)(2,1)}, bf16[512,128]{1,0:T(8,128)(2,1)}, bf16[512,128]{1,0:T(8,128)(2,1)}) custom-call(s32[1]{0:T(128)} %copy.23.length_ref, bf16[512,2048]{1,0:T(8,128)(2,1)} %bitcast.31, f32[1,2048]{1,0:T(1,128)} %bitcast.36, bf16[64,1024]{1,0:T(8,128)(2,1)} %wq_ref.1, bf16[64,128]{1,0:T(8,128)(2,1)} %wk_ref.1, ...), custom_call_target="tpu_custom_call" | custom-call | tf_op jit(solution)/shard_map/front/pallas_call | solution.py:689
  94.7 0.0 copy-done.4
  94.7 0.0 copy-done.5
  94.7 0.3 convert_reduce_fusion
  95.1 0.1 convolution_multiply_fusion
  95.2 0.7 pad_maximum_fusion.2.map_ref
  95.9 102.4 %serve.1 = (bf16[4,4,2,48,2048]{4,3,2,1,0:T(8,128)(2,1)}, bf16[2,4,512,384]{3,2,1,0:T(8,128)(2,1)}) custom-call(bf16[128,2048]{1,0:T(8,128)(2,1)} %get-tuple-element.9.rows_ref, f32[4,64,128]{2,1,0:T(8,128)} %pad_maximum_fusion.2.map_ref, bf16[1,2048,768]{2,1,0:T(8,128)(2,1)} %gate_ref.1, bf16[1,2048,768]{2,1,0:T(8,128)(2,1)} %up_ref.1, ...), custom_call_target="tpu_custom_call" | custom-call | tf_op jit(solution)/shard_map/serve/pallas_call | solution.py:282
  198.2 0.0 copy-start
  198.3 90.0 %combine.1 = bf16[128,2048]{1,0:T(8,128)(2,1)} custom-call(bf16[4,4,2,48,2048]{4,3,2,1,0:T(8,128)(2,1)} %get-tuple-element.10.made_ref, bf16[2,4,512,384]{3,2,1,0:T(8,128)(2,1)} %get-tuple-element.11.weigh_ref, bf16[128,2048]{1,0:T(8,128)(2,1)} %get-tuple-element.12.base_ref), custom_call_target="tpu_custom_call" | custom-call | tf_op jit(solution)/shard_map/combine/pallas_call | solution.py:409
  288.3 0.0 copy-done
  288.3 0.0 copy-start.3
  288.4 0.0 copy-start.2
  288.4 0.0 copy-start.1
  288.4 5.0 %select_bitcast_fusion = (bf16[1,4608,128]{2,1,0:T(8,128)(2,1)}, bf16[1,4608,128]{2,1,0:T(8,128)(2,1)}) fusion(bf16[4096,128]{1,0:T(8,128)(2,1)} %bitcast.29, pred[4608]{0:T(1024)(128)(4,1)S(1)} %iota_compare_fusion.3, bf16[4096,128]{1,0:T(8,128)(2,1)S(1)} %bitcast.28), kind=kLoop, calls=%fused_computation | loop fusion | flops 1179648 | bytes 4461056 | tf_op jit(solution)/shard_map/broadcast_in_dim | solution.py:779
  293.4 0.0 copy-done.3
  293.4 1.8 dynamic_update_slice.8
  295.2 0.0 copy-done.2
  295.2 1.8 dynamic_update_slice.9
  297.0 0.0 copy-done.1
  297.0 0.8 copy.24
  (3 shorter events, 0.0 us)
Async XLA Ops:
  3.3 91.4 %copy-start.4 = (s32[1,128,8]{1,2,0:T(8,128)S(1)}, s32[1,128,8]{1,2,0:T(8,128)}, u32[]{:S(2)}) copy-start(s32[1,128,8]{1,2,0:T(8,128)} %param.29) | copy-start | bytes 12292
  3.3 91.4 %copy-start.5 = (f32[1,128,8]{1,2,0:T(8,128)S(1)}, f32[1,128,8]{1,2,0:T(8,128)}, u32[]{:S(2)}) copy-start(f32[1,128,8]{1,2,0:T(8,128)} %param.30) | copy-start | bytes 12292
  198.2 90.1 %copy-start = (bf16[1,4096,128]{2,1,0:T(8,128)(2,1)S(1)}, bf16[1,4096,128]{2,1,0:T(8,128)(2,1)}, u32[]{:S(2)}) copy-start(bf16[1,4096,128]{2,1,0:T(8,128)(2,1)} %ck_ref.1) | copy-start | bytes 3145732
  288.3 5.1 %copy-start.3 = (bf16[512,128]{1,0:T(8,128)(2,1)S(1)}, bf16[512,128]{1,0:T(8,128)(2,1)}, u32[]{:S(2)}) copy-start(bf16[512,128]{1,0:T(8,128)(2,1)} %get-tuple-element.13) | copy-start | bytes 393220
  288.4 6.8 %copy-start.2 = (bf16[512,128]{1,0:T(8,128)(2,1)S(1)}, bf16[512,128]{1,0:T(8,128)(2,1)}, u32[]{:S(2)}) copy-start(bf16[512,128]{1,0:T(8,128)(2,1)} %get-tuple-element.14) | copy-start | bytes 393220
  288.4 8.6 %copy-start.1 = (bf16[128,2048]{1,0:T(8,128)(2,1)S(1)}, bf16[128,2048]{1,0:T(8,128)(2,1)}, u32[]{:S(2)}) copy-start(bf16[128,2048]{1,0:T(8,128)(2,1)} %combine.1) | copy-start | bytes 1572868

commit v4 on v3

--- a/solution.py
+++ b/solution.py
@@ -729,13 +729,32 @@
     return jnp.concatenate([cosine, cosine], axis=1), jnp.concatenate([-sine, sine], axis=1)
 
 
-def append(cache, fresh, length):
-    span = cache.shape[0] + fresh.shape[0]
-    padded = jnp.concatenate([cache, jnp.zeros_like(fresh)], axis=0)
-    kept_rows = jnp.where(
-        (jnp.arange(span, dtype=jnp.int32) < length)[:, None], padded, jnp.zeros_like(padded)
-    )
-    return lax.dynamic_update_slice(kept_rows, fresh, (length, jnp.zeros((), jnp.int32)))
+def append_body(length_ref, ck_ref, cv_ref, fk_ref, fv_ref, ko_ref, vo_ref, moved):
+    length = length_ref[0]
+    cached = ck_ref.shape[1]
+    fresh = fk_ref.shape[0]
+    row = lax.broadcasted_iota(jnp.int32, ck_ref.shape[1:], 0)
+    for cache, new, out in ((ck_ref, fk_ref, ko_ref), (cv_ref, fv_ref, vo_ref)):
+        moved[...] = jnp.zeros_like(moved)
+        moved[pl.ds(length, fresh), :] = new[...].astype(jnp.float32)
+        tail = moved[...].astype(jnp.bfloat16)
+        out[0, 0:cached] = jnp.where(row < length, cache[0], tail[0:cached])
+        out[0, cached:] = tail[cached:]
+
+
+def append(cache_keys, cache_values, fresh_keys, fresh_values, length):
+    _, cached, width = cache_keys.shape
+    span = cached + fresh_keys.shape[0]
+    vmem = pl.BlockSpec(memory_space=pltpu.VMEM)
+    return pl.pallas_call(
+        append_body,
+        out_shape=(jax.ShapeDtypeStruct((1, span, width), jnp.bfloat16),) * 2,
+        in_specs=[pl.BlockSpec(memory_space=pltpu.SMEM)] + [vmem] * 4,
+        out_specs=(vmem, vmem),
+        scratch_shapes=[pltpu.VMEM((span, width), jnp.float32)],
+        compiler_params=pltpu.CompilerParams(vmem_limit_bytes=32 << 20),
+        name="append",
+    )(length, cache_keys, cache_values, fresh_keys, fresh_values)
 
 
 def body(
@@ -774,9 +793,10 @@
     maps = routing_maps(routes, expert_gates[0], experts, groups)
     made, weigh = serve(moe_in, maps, w_gate, w_up, w_down, capacity)
     result_rows = combine(made, weigh, after_attn)
-    keys_out = append(cache_keys[0], fresh_keys, length)
-    values_out = append(cache_values[0], fresh_values, length)
-    return (result_rows[None], keys_out[None], values_out[None])
+    keys_out, values_out = append(
+        cache_keys, cache_values, fresh_keys, fresh_values, cache_len
+    )
+    return (result_rows[None], keys_out, values_out)
 
 
 def solution(mesh):

time: 302 us -> 298 us (0.987)
  other arithmetic: 8.05 us -> 3.02 us
    broadcast_in_dim x1 -> x0, other arithmetic: 5.03 us -> none  [body(): return (result_rows[None], keys_out[None], values_out[None])]
    dynamic_update_slice x2 -> x0, local copies, waits for them, and re-layouts: 3.55 us -> none  [append(): lax.dynamic_update_slice(kept_rows, fresh, (length, jnp.zeros((), jnp.int...]
where the time goes in v4:
time: 298 us; the launch traced here: 294 us
  Pallas kernels  286 us (96%)
  local copies, waits for them, and re-layouts  3.13 us (1%)
  other arithmetic  3.02 us (1%)
    pallas_call x1, Pallas kernels, serve(): pl.pallas_call(serve_body, out_shape=(jax.ShapeDtypeStruct((4, 4, 2, grou...  102 us
    pallas_call x1, Pallas kernels, front(): pl.pallas_call(functools.partial(front_body, width ** (-0.5) * math.log2(...  91.4 us
    pallas_call x1, Pallas kernels, combine(): pl.pallas_call(combine_body, out_shape=jax.ShapeDtypeStruct(base.shape, b...  90.1 us

profile of v4, /device:TPU:26, one launch (start us, length us, event | category | flops | bytes accessed | tf_op | source)
XLA Modules:
  0.0 294.0 jit_solution(15811710890437273263)
XLA Ops:
  1.3 1.0 fusion
  2.3 0.0 copy-start.4
  2.3 0.0 copy-start.5
  2.3 1.0 pad_maximum_fusion
  3.3 91.4 %front.1 = (bf16[128,2048]{1,0:T(8,128)(2,1)}, bf16[128,2048]{1,0:T(8,128)(2,1)}, bf16[512,128]{1,0:T(8,128)(2,1)}, bf16[512,128]{1,0:T(8,128)(2,1)}) custom-call(s32[1]{0:T(128)} %copy.21.length_ref, bf16[512,2048]{1,0:T(8,128)(2,1)} %bitcast.17, f32[1,2048]{1,0:T(1,128)} %bitcast.20, bf16[64,1024]{1,0:T(8,128)(2,1)} %wq_ref.1, bf16[64,128]{1,0:T(8,128)(2,1)} %wk_ref.1, ...), custom_call_target="tpu_custom_call" | custom-call | tf_op jit(solution)/shard_map/front/pallas_call | solution.py:689
  94.7 0.0 copy-done.4
  94.7 0.0 copy-done.5
  94.7 0.3 convert_reduce_fusion
  95.1 0.1 convolution_multiply_fusion
  95.2 0.7 pad_maximum_fusion.2.map_ref
  95.9 102.3 %serve.1 = (bf16[4,4,2,48,2048]{4,3,2,1,0:T(8,128)(2,1)}, bf16[2,4,512,384]{3,2,1,0:T(8,128)(2,1)}) custom-call(bf16[128,2048]{1,0:T(8,128)(2,1)} %get-tuple-element.11.rows_ref, f32[4,64,128]{2,1,0:T(8,128)} %pad_maximum_fusion.2.map_ref, bf16[1,2048,768]{2,1,0:T(8,128)(2,1)} %gate_ref.1, bf16[1,2048,768]{2,1,0:T(8,128)(2,1)} %up_ref.1, ...), custom_call_target="tpu_custom_call" | custom-call | tf_op jit(solution)/shard_map/serve/pallas_call | solution.py:282
  198.2 0.0 copy-start
  198.3 0.0 copy-start.2
  198.3 0.0 copy-start.3
  198.3 90.1 %combine.1 = bf16[128,2048]{1,0:T(8,128)(2,1)} custom-call(bf16[4,4,2,48,2048]{4,3,2,1,0:T(8,128)(2,1)} %get-tuple-element.12.made_ref, bf16[2,4,512,384]{3,2,1,0:T(8,128)(2,1)} %get-tuple-element.13.weigh_ref, bf16[128,2048]{1,0:T(8,128)(2,1)} %get-tuple-element.14.base_ref), custom_call_target="tpu_custom_call" | custom-call | tf_op jit(solution)/shard_map/combine/pallas_call | solution.py:409
  288.4 0.0 copy-done
  288.4 0.0 copy-done.2
  288.4 0.0 copy-done.3
  288.4 0.0 copy-start.1
  288.4 1.2 copy-done.1
  289.6 2.5 append.1
  292.2 1.9 copy.22
  (2 shorter events, 0.0 us)
Async XLA Ops:
  2.3 92.4 %copy-start.4 = (s32[1,128,8]{1,2,0:T(8,128)S(1)}, s32[1,128,8]{1,2,0:T(8,128)}, u32[]{:S(2)}) copy-start(s32[1,128,8]{1,2,0:T(8,128)} %param.29) | copy-start | bytes 12292
  2.3 92.4 %copy-start.5 = (f32[1,128,8]{1,2,0:T(8,128)S(1)}, f32[1,128,8]{1,2,0:T(8,128)}, u32[]{:S(2)}) copy-start(f32[1,128,8]{1,2,0:T(8,128)} %param.30) | copy-start | bytes 12292
  198.2 90.1 %copy-start = (bf16[1,4096,128]{2,1,0:T(8,128)(2,1)S(1)}, bf16[1,4096,128]{2,1,0:T(8,128)(2,1)}, u32[]{:S(2)}) copy-start(bf16[1,4096,128]{2,1,0:T(8,128)(2,1)} %ck_ref.3) | copy-start | bytes 3145732
  198.3 90.1 %copy-start.2 = (bf16[512,128]{1,0:T(8,128)(2,1)S(1)}, bf16[512,128]{1,0:T(8,128)(2,1)}, u32[]{:S(2)}) copy-start(bf16[512,128]{1,0:T(8,128)(2,1)} %get-tuple-element.15.fk_ref) | copy-start | bytes 393220
  198.3 90.1 %copy-start.3 = (bf16[512,128]{1,0:T(8,128)(2,1)S(1)}, bf16[512,128]{1,0:T(8,128)(2,1)}, u32[]{:S(2)}) copy-start(bf16[512,128]{1,0:T(8,128)(2,1)} %get-tuple-element.16.fv_ref) | copy-start | bytes 393220
  288.4 1.2 copy-start.1

commit v5 on v4

--- a/solution.py
+++ b/solution.py
@@ -225,24 +225,40 @@
                     outbox[q].at[spot], slot, c_send.at[q, step], c_recv.at[q, spot], peer
                 ).wait_recv()
 
-    cut = chunks[EARLY][0]
+    early = chunks[EARLY][0]
     hidden_width = w_gate.shape[1]
     arrive(range(EARLY))
     for load in loads:
         load.wait()
 
     def begin(r, carry):
-        x = inbox[r, :, :, :, 0:cut].reshape(8 * group, cut)
+        x = inbox[r, :, :, :, 0:early].reshape(8 * group, early)
         partial[r, :, 0:hidden_width] = jnp.dot(
-            x, w_gate[0:cut, :], preferred_element_type=jnp.float32
+            x, w_gate[0:early, :], preferred_element_type=jnp.float32
         )
         partial[r, :, hidden_width:] = jnp.dot(
-            x, w_up[0:cut, :], preferred_element_type=jnp.float32
+            x, w_up[0:early, :], preferred_element_type=jnp.float32
         )
         return carry
 
     lax.fori_loop(0, 4, begin, 0)
-    arrive(range(EARLY, COUNT))
+    for q in range(EARLY, COUNT - 1):
+        arrive((q,))
+        low, high = chunks[q][0], chunks[q + 1][0]
+
+        def resume(r, carry, low=low, high=high):
+            x = inbox[r, :, :, :, low:high].reshape(8 * group, high - low)
+            partial[r, :, 0:hidden_width] += jnp.dot(
+                x, w_gate[low:high, :], preferred_element_type=jnp.float32
+            )
+            partial[r, :, hidden_width:] += jnp.dot(
+                x, w_up[low:high, :], preferred_element_type=jnp.float32
+            )
+            return carry
+
+        lax.fori_loop(0, 4, resume, 0)
+    arrive((COUNT - 1,))
+    cut = chunks[COUNT - 1][0]
 
     def expert(r, carry):
         x = inbox[r, :, :, :, cut:].reshape(8 * group, inbox.shape[-1] - cut)
@@ -565,13 +581,8 @@
     second_stage(1)
     handed(0)
 
-    def project(i, carry):
-        rows = pl.ds(i * block, block)
-        flat = weights[...].reshape(normed.shape[1], weights.shape[-1])
-        proj[rows, :] = jnp.dot(normed[rows, :], flat, preferred_element_type=jnp.float32)
-        return carry
-
-    lax.fori_loop(0, 4, project, 0)
+    flat = weights[...].reshape(normed.shape[1], weights.shape[-1])
+    proj[...] = jnp.dot(normed[...], flat, preferred_element_type=jnp.float32)
 
     def turned(values, gain):
         factor = lax.rsqrt(jnp.mean(values * values, axis=-1, keepdims=True) + EPS)

time: 298 us -> 295 us (0.990)
  Pallas kernels: 286 us -> 283 us
where the time goes in v5:
time: 295 us; the launch traced here: 291 us
  Pallas kernels  283 us (96%)
  local copies, waits for them, and re-layouts  3.13 us (1%)
  other arithmetic  3.02 us (1%)
    pallas_call x1, Pallas kernels, serve(): pl.pallas_call(serve_body, out_shape=(jax.ShapeDtypeStruct((4, 4, 2, grou...  100 us
    pallas_call x1, Pallas kernels, front(): pl.pallas_call(functools.partial(front_body, width ** (-0.5) * math.log2(...  90.5 us
    pallas_call x1, Pallas kernels, combine(): pl.pallas_call(combine_body, out_shape=jax.ShapeDtypeStruct(base.shape, b...  90.1 us

profile of v5, /device:TPU:26, one launch (start us, length us, event | category | flops | bytes accessed | tf_op | source)
XLA Modules:
  0.0 290.8 jit_solution(6250491238365183732)
XLA Ops:
  1.3 1.0 fusion
  2.3 0.0 copy-start.4
  2.3 0.0 copy-start.5
  2.3 1.0 pad_maximum_fusion
  3.3 90.5 %front.1 = (bf16[128,2048]{1,0:T(8,128)(2,1)}, bf16[128,2048]{1,0:T(8,128)(2,1)}, bf16[512,128]{1,0:T(8,128)(2,1)}, bf16[512,128]{1,0:T(8,128)(2,1)}) custom-call(s32[1]{0:T(128)} %copy.21.length_ref, bf16[512,2048]{1,0:T(8,128)(2,1)} %bitcast.17, f32[1,2048]{1,0:T(1,128)} %bitcast.20, bf16[64,1024]{1,0:T(8,128)(2,1)} %wq_ref.1, bf16[64,128]{1,0:T(8,128)(2,1)} %wk_ref.1, ...), custom_call_target="tpu_custom_call" | custom-call | tf_op jit(solution)/shard_map/front/pallas_call | solution.py:700
  93.8 0.0 copy-done.4
  93.8 0.0 copy-done.5
  93.8 0.3 convert_reduce_fusion
  94.2 0.1 convolution_multiply_fusion
  94.3 0.7 pad_maximum_fusion.2.map_ref
  95.0 100.0 %serve.1 = (bf16[4,4,2,48,2048]{4,3,2,1,0:T(8,128)(2,1)}, bf16[2,4,512,384]{3,2,1,0:T(8,128)(2,1)}) custom-call(bf16[128,2048]{1,0:T(8,128)(2,1)} %get-tuple-element.11.rows_ref, f32[4,64,128]{2,1,0:T(8,128)} %pad_maximum_fusion.2.map_ref, bf16[1,2048,768]{2,1,0:T(8,128)(2,1)} %gate_ref.1, bf16[1,2048,768]{2,1,0:T(8,128)(2,1)} %up_ref.1, ...), custom_call_target="tpu_custom_call" | custom-call | tf_op jit(solution)/shard_map/serve/pallas_call | solution.py:298
  195.0 0.0 copy-start
  195.0 0.0 copy-start.2
  195.0 0.0 copy-start.3
  195.0 90.1 %combine.1 = bf16[128,2048]{1,0:T(8,128)(2,1)} custom-call(bf16[4,4,2,48,2048]{4,3,2,1,0:T(8,128)(2,1)} %get-tuple-element.12.made_ref, bf16[2,4,512,384]{3,2,1,0:T(8,128)(2,1)} %get-tuple-element.13.weigh_ref, bf16[128,2048]{1,0:T(8,128)(2,1)} %get-tuple-element.14.base_ref), custom_call_target="tpu_custom_call" | custom-call | tf_op jit(solution)/shard_map/combine/pallas_call | solution.py:425
  285.1 0.0 copy-done
  285.1 0.0 copy-done.2
  285.1 0.0 copy-done.3
  285.1 0.0 copy-start.1
  285.1 1.2 copy-done.1
  286.4 2.5 append.1
  288.9 1.9 copy.22
  (2 shorter events, 0.0 us)
Async XLA Ops:
  2.3 91.5 %copy-start.4 = (s32[1,128,8]{1,2,0:T(8,128)S(1)}, s32[1,128,8]{1,2,0:T(8,128)}, u32[]{:S(2)}) copy-start(s32[1,128,8]{1,2,0:T(8,128)} %param.29) | copy-start | bytes 12292
  2.3 91.5 %copy-start.5 = (f32[1,128,8]{1,2,0:T(8,128)S(1)}, f32[1,128,8]{1,2,0:T(8,128)}, u32[]{:S(2)}) copy-start(f32[1,128,8]{1,2,0:T(8,128)} %param.30) | copy-start | bytes 12292
  195.0 90.1 %copy-start = (bf16[1,4096,128]{2,1,0:T(8,128)(2,1)S(1)}, bf16[1,4096,128]{2,1,0:T(8,128)(2,1)}, u32[]{:S(2)}) copy-start(bf16[1,4096,128]{2,1,0:T(8,128)(2,1)} %ck_ref.3) | copy-start | bytes 3145732
  195.0 90.1 %copy-start.2 = (bf16[512,128]{1,0:T(8,128)(2,1)S(1)}, bf16[512,128]{1,0:T(8,128)(2,1)}, u32[]{:S(2)}) copy-start(bf16[512,128]{1,0:T(8,128)(2,1)} %get-tuple-element.15.fk_ref) | copy-start | bytes 393220
  195.0 90.1 %copy-start.3 = (bf16[512,128]{1,0:T(8,128)(2,1)S(1)}, bf16[512,128]{1,0:T(8,128)(2,1)}, u32[]{:S(2)}) copy-start(bf16[512,128]{1,0:T(8,128)(2,1)} %get-tuple-element.16.fv_ref) | copy-start | bytes 393220
  285.1 1.2 copy-start.1
